TPU v7x, 128 devices: a whole 4x4x4 slice. The times are simulated.
128 devices in a mesh: src: 8 (over z, core), tgt: 16 (over x, y).
Axes of the slice: x: 4, y: 4, z: 4, core: 2. Of those that a mesh axis runs over, the one named last changes fastest.
Arguments:
- src_points: bfloat16 [64, 256, 128], P('src', 'tgt')
- tgt_points: bfloat16 [128, 256, 128], P('tgt', 'src'), may hold values from -1.5 to 1.5
- src_mass: bfloat16 [64, 256], P('src', 'tgt'), may hold values from 0.099609375 to 10
- tgt_mass: bfloat16 [128, 256], P('tgt', 'src'), may hold values from 0.099609375 to 10
- src_potential: bfloat16 [64, 256], P('src', 'tgt'), may hold values from -452 to 452
- tgt_potential: bfloat16 [128, 256], P('tgt', 'src'), may hold values from -452 to 452
- src_counts: int32 [64], P('src'), may hold values from 16 to 256, as said below
- tgt_counts: int32 [128], P('tgt'), may hold values from 16 to 256, as said below
- keep: int32 [64, 128], P('src', 'tgt'), may hold values from 0 to 1, as said below
Outputs:
- images: float32 [64, 256, 128], P('src', 'tgt')
- src_final: float32 [64, 256], P('src', 'tgt')
- tgt_final: float32 [128, 256], P('tgt', 'src')
Inputs may be any that keep to these rules, and one draw needn't show every extreme that they name: `keep`: every source block keeps at least one target block and every target block is kept by at least one source block. `src_counts`: some source block is full. `tgt_counts`: some target block is full.
All inputs are finite; a program needn't handle non-finite values.
Results may differ from a plain program's by a relative error of at most 0.0003.
Values may be sent and summed in bfloat16 or wider, within the bound.
A program may use at most 64 MiB of HBM per device.

v0:
```python
import jax
import jax.numpy as jnp
from jax import lax
from jax.sharding import PartitionSpec as P

ITERS = 4


EPSILON = 0.1
FLOOR = -1e30


def row_lse(peak, total):
    top = lax.pmax(peak, "tgt")
    whole = (top, lax.psum(total * jnp.exp(peak - top), "tgt"))
    return whole


def col_lse(peak, total):
    top = lax.pmax(peak, "src")
    whole = (top, lax.psum(total * jnp.exp(peak - top), "src"))
    return whole


def on_device(
    src_points,
    tgt_points,
    src_mass,
    tgt_mass,
    src_potential,
    tgt_potential,
    src_counts,
    tgt_counts,
    keep,
):
    xs_all, a_mass, f_start = (
        lax.all_gather(src_points, "tgt", axis=1, tiled=True),
        lax.all_gather(src_mass, "tgt", axis=1, tiled=True),
        lax.all_gather(src_potential, "tgt", axis=1, tiled=True),
    )
    ys_all, b_mass, g_start = (
        lax.all_gather(tgt_points, "src", axis=1, tiled=True),
        lax.all_gather(tgt_mass, "src", axis=1, tiled=True),
        lax.all_gather(tgt_potential, "src", axis=1, tiled=True),
    )
    sb, blk, width = xs_all.shape
    tb = ys_all.shape[0]
    ncols = tb * blk
    group = min(sb, max(1, 512 // blk))
    steps_n = sb // group
    rows = group * blk
    x_flat = xs_all.reshape(sb * blk, width)
    y_flat = ys_all.reshape(ncols, width)
    x_wide = x_flat.astype(jnp.float32)
    y_wide = y_flat.astype(jnp.float32)
    x_half = (0.5 * jnp.sum(x_wide * x_wide, axis=1)).reshape(steps_n, rows)
    y_half = 0.5 * jnp.sum(y_wide * y_wide, axis=1)
    slots = jnp.arange(blk, dtype=jnp.int32)
    src_live = (slots[None, :] < src_counts[:, None]).reshape(steps_n, rows)
    tgt_live = (slots[None, :] < tgt_counts[:, None]).reshape(-1)
    log_a = jnp.log(a_mass.astype(jnp.float32)).reshape(steps_n, rows)
    log_b = jnp.log(b_mass.astype(jnp.float32)).reshape(-1)
    keep_grp = jnp.repeat(keep > 0, blk, axis=1).reshape(steps_n, group, ncols)
    x_grp = x_flat.reshape(steps_n, rows, width)

    def tile(x, xh, blocks):
        cost = (
            xh[:, None]
            + y_half[None, :]
            - lax.dot_general(
                x, y_flat, (((1,), (1,)), ((), ())), preferred_element_type=jnp.float32
            )
        )
        return (cost, jnp.repeat(blocks, blk, axis=0))

    def row_scores(cost, pair, g_now):
        row_ok = pair & tgt_live[None, :]
        scored = jnp.where(row_ok, log_b[None, :] + (g_now[None, :] - cost) / EPSILON, FLOOR)
        return (scored, row_ok)

    def local_rows(scored, row_ok):
        peak = jnp.max(scored, axis=1)
        weights = jnp.where(row_ok, jnp.exp(scored - peak[:, None]), 0.0)
        return (peak, weights)

    f_cur = f_start.astype(jnp.float32).reshape(-1)
    g_cur = g_start.astype(jnp.float32).reshape(-1)
    for step in range(ITERS):
        sweep_g_now = g_cur

        def visit(carry, item):
            colmax, colsum = carry
            x, xh, live, lga, fpart, blocks = item
            cost, pair = tile(x, xh, blocks)
            scored, row_ok = row_scores(cost, pair, sweep_g_now)
            peak, weights = local_rows(scored, row_ok)
            col_ok = pair & live[:, None]
            colterm = jnp.where(col_ok, lga[:, None] + (fpart[:, None] - cost) / EPSILON, FLOOR)
            top = jnp.maximum(colmax, jnp.max(colterm, axis=0))
            colsum = colsum * jnp.exp(colmax - top) + jnp.sum(
                jnp.where(col_ok, jnp.exp(colterm - top[None, :]), 0.0), axis=0
            )
            return ((top, colsum), (peak, jnp.sum(weights, axis=1)))

        start = (jnp.full((ncols,), FLOOR, jnp.float32), jnp.zeros((ncols,), jnp.float32))
        (colmax, colsum), (rpeak, rtotal) = lax.scan(
            visit, start, (x_grp, x_half, src_live, log_a, f_cur.reshape(steps_n, rows), keep_grp)
        )
        whole_rows = row_lse(rpeak.reshape(-1), rtotal.reshape(-1))
        whole_cols = col_lse(colmax, colsum)
        f_new = -EPSILON * (whole_rows[0] + jnp.log(whole_rows[1]))
        g_new = -EPSILON * (whole_cols[0] + jnp.log(whole_cols[1]))
        f_new, g_new = (f_new, g_new)
        f_cur = 0.5 * (f_cur + f_new)
        g_cur = 0.5 * (g_cur + g_new)
    ntgt = lax.axis_size("tgt")
    nsrc = lax.axis_size("src")
    src_piece = blk // ntgt
    tgt_piece = blk // nsrc
    src_start = lax.axis_index("tgt") * src_piece
    tgt_start = lax.axis_index("src") * tgt_piece

    def measure(carry, item):
        x, xh, blocks = item
        cost, pair = tile(x, xh, blocks)
        scored, row_ok = row_scores(cost, pair, g_cur)
        peak, weights = local_rows(scored, row_ok)
        return (carry, (peak, jnp.sum(weights, axis=1)))

    unused, (peak, total) = lax.scan(measure, jnp.zeros((), jnp.float32), (x_grp, x_half, keep_grp))
    top, whole_total = row_lse(peak.reshape(-1), total.reshape(-1))
    top_grp = top.reshape(steps_n, rows)
    total_grp = whole_total.reshape(steps_n, rows)

    def project(carry, item):
        x, xh, blocks, top_rows, total_rows = item
        cost, pair = tile(x, xh, blocks)
        scored, row_ok = row_scores(cost, pair, g_cur)
        weights = jnp.where(row_ok, jnp.exp(scored - top_rows[:, None]), 0.0)
        moved = jnp.dot(weights, y_wide, precision=lax.Precision.HIGHEST) / total_rows[:, None]
        return (carry, moved)

    unused, moved = lax.scan(
        project, jnp.zeros((), jnp.float32), (x_grp, x_half, keep_grp, top_grp, total_grp)
    )
    images = lax.psum_scatter(moved.reshape(sb, blk, width), "tgt", scatter_dimension=1, tiled=True)
    src_final = lax.dynamic_slice_in_dim(f_cur.reshape(sb, blk), src_start, src_piece, 1)
    tgt_final = lax.dynamic_slice_in_dim(g_cur.reshape(tb, blk), tgt_start, tgt_piece, 1)
    return (images, src_final, tgt_final)


def solution(mesh):
    return jax.shard_map(
        on_device,
        mesh=mesh,
        in_specs=(
            P("src", "tgt", None),
            P("tgt", "src", None),
            P("src", "tgt"),
            P("tgt", "src"),
            P("src", "tgt"),
            P("tgt", "src"),
            P("src"),
            P("tgt"),
            P("src", "tgt"),
        ),
        out_specs=(P("src", "tgt", None), P("src", "tgt"), P("tgt", "src")),
        check_vma=False,
    )
```

profile of v0, /device:TPU:1, one launch (start us, length us, event | category | flops | bytes accessed | tf_op | source)
XLA Modules:
  0.0 865.6 jit_solution(17146617949855784348)
XLA Ops:
  7.3 15.9 %all_gather.23 = bf16[8,256,128]{2,1,0:T(8,128)(2,1)S(1)} all-gather(bf16[8,32,128]{2,1,0:T(8,128)(2,1)} %param.22), channel_id=1, replica_groups=mesh['src'=8,'tgt'=16] {'src'}, dimensions={1}, use_global_device_ids=true | all-gather | bytes 589824 | tf_op jit(solution)/shard_map/all_gather | solution.py:42
  23.7 20.0 %all_gather.22 = bf16[8,256,128]{2,1,0:T(8,128)(2,1)S(1)} all-gather(bf16[8,16,128]{2,1,0:T(8,128)(2,1)} %param.21), channel_id=1, replica_groups=mesh['src'=8,'tgt'=16] {'tgt'}, dimensions={1}, use_global_device_ids=true | all-gather | bytes 557056 | tf_op jit(solution)/shard_map/all_gather | solution.py:37
  44.0 17.1 %all-gather = bf16[8,32,8]{1,2,0:T(8,128)(2,1)S(1)} all-gather(bf16[1,32,8]{1,2,0:T(8,128)(2,1)} %bitcast.488), channel_id=1, replica_groups=mesh['src'=8,'tgt'=16] {'src'}, dimensions={0}, use_global_device_ids=true | all-gather | bytes 4608 | tf_op jit(solution)/shard_map/all_gather | solution.py:43
  62.0 16.8 %all-gather.2 = bf16[16,16,8]{1,2,0:T(8,128)(2,1)S(1)} all-gather(bf16[1,16,8]{1,2,0:T(8,128)(2,1)} %bitcast.489), channel_id=1, replica_groups=mesh['src'=8,'tgt'=16] {'tgt'}, dimensions={0}, use_global_device_ids=true | all-gather | bytes 4352 | tf_op jit(solution)/shard_map/all_gather | solution.py:38
  79.1 16.1 %all-gather.3 = bf16[16,16,8]{1,2,0:T(8,128)(2,1)S(1)} all-gather(bf16[1,16,8]{1,2,0:T(8,128)(2,1)S(1)} %bitcast.490), channel_id=1, replica_groups=mesh['src'=8,'tgt'=16] {'tgt'}, dimensions={0}, use_global_device_ids=true | all-gather | bytes 4352 | tf_op jit(solution)/shard_map/all_gather | solution.py:39
  95.4 22.4 %all-gather.1 = bf16[8,32,8]{1,2,0:T(8,128)(2,1)S(1)} all-gather(bf16[1,32,8]{1,2,0:T(8,128)(2,1)S(1)} %bitcast.491), channel_id=1, replica_groups=mesh['src'=8,'tgt'=16] {'src'}, dimensions={0}, use_global_device_ids=true | all-gather | bytes 4608 | tf_op jit(solution)/shard_map/all_gather | solution.py:44
  117.9 39.2 %while.94 = (s32[]{:T(128)}, f32[2048]{0:T(1024)S(1)}, f32[2048]{0:T(1024)S(1)}, f32[4,512]{1,0:T(4,128)S(1)}, f32[4,512]{1,0:T(4,128)S(1)}, /*index=5*/pred[4,2...) while((s32[]{:T(128)}, f32[2048]{0:T(1024)S(1)}, ...), condition=%wide.region_7.8_spmd.clone, body=%wide.region_2.7_spmd.clone.sunk | while | flops 302001152 | bytes 9304300 | solution.py:106
  121.9 5.6 fusion.143
  127.9 3.8 fusion.142
  131.7 5.6 fusion.143
  137.7 3.8 fusion.142
  141.6 5.6 fusion.143
  147.5 3.8 fusion.142
  151.4 5.6 fusion.143
  157.2 31.5 %pmax.64 = f32[2048]{0:T(1024)S(1)} all-reduce(f32[2048]{0:T(1024)S(1)} %bitcast.455), channel_id=1, replica_groups=mesh['src'=8,'tgt'=16] {'tgt'}, use_global_device_ids=true, to_apply=%region_10.11 | all-reduce | flops 2048 | bytes 16384 | tf_op jit(solution)/shard_map/pmax | solution.py:14
  188.7 29.2 %psum.64 = f32[2048]{0:T(1024)S(1)} all-reduce(f32[2048]{0:T(1024)S(1)} %exponential_multiply_fusion.7), channel_id=1, replica_groups=mesh['src'=8,'tgt'=16] {'tgt'}, use_global_device_ids=true, to_apply=%region_11.12 | all-reduce | flops 2048 | bytes 16384 | tf_op jit(solution)/shard_map/psum | solution.py:15
  217.9 26.1 %pmax.63 = f32[2048]{0:T(1024)S(1)} all-reduce(f32[2048]{0:T(1024)S(1)} %get-tuple-element.468), channel_id=1, replica_groups=mesh['src'=8,'tgt'=16] {'src'}, use_global_device_ids=true, to_apply=%region_8.9 | all-reduce | flops 2048 | bytes 16384 | tf_op jit(solution)/shard_map/pmax | solution.py:20
  244.0 12.7 %psum.63 = f32[2048]{0:T(1024)S(1)} all-reduce(f32[2048]{0:T(1024)S(1)} %exponential_multiply_fusion.8), channel_id=1, replica_groups=mesh['src'=8,'tgt'=16] {'src'}, use_global_device_ids=true, to_apply=%region_9.10 | all-reduce | flops 2048 | bytes 16384 | tf_op jit(solution)/shard_map/psum | solution.py:21
  256.8 39.2 %while.95 = (s32[]{:T(128)}, f32[2048]{0:T(1024)S(1)}, f32[2048]{0:T(1024)S(1)}, f32[4,512]{1,0:T(4,128)S(1)}, f32[4,512]{1,0:T(4,128)S(1)}, /*index=5*/pred[4,2...) while((s32[]{:T(128)}, f32[2048]{0:T(1024)S(1)}, ...), condition=%wide.region_17.18_spmd.clone, body=%wide.region_12.17_spmd.clone.sunk | while | flops 302001152 | bytes 9287916 | solution.py:106
  257.0 3.8 fusion.146
  260.8 5.6 fusion.147
  266.8 3.8 fusion.146
  270.6 5.6 fusion.147
  276.6 3.8 fusion.146
  280.4 5.6 fusion.147
  286.4 3.8 fusion.146
  290.2 5.6 fusion.147
  296.0 30.7 %pmax.66 = f32[2048]{0:T(1024)S(1)} all-reduce(f32[2048]{0:T(1024)S(1)} %bitcast.457), channel_id=1, replica_groups=mesh['src'=8,'tgt'=16] {'tgt'}, use_global_device_ids=true, to_apply=%region_20.21 | all-reduce | flops 2048 | bytes 16384 | tf_op jit(solution)/shard_map/pmax | solution.py:14
  326.8 29.0 %psum.66 = f32[2048]{0:T(1024)S(1)} all-reduce(f32[2048]{0:T(1024)S(1)} %exponential_multiply_fusion.5), channel_id=1, replica_groups=mesh['src'=8,'tgt'=16] {'tgt'}, use_global_device_ids=true, to_apply=%region_21.22 | all-reduce | flops 2048 | bytes 16384 | tf_op jit(solution)/shard_map/psum | solution.py:15
  355.8 26.9 %pmax.65 = f32[2048]{0:T(1024)S(1)} all-reduce(f32[2048]{0:T(1024)S(1)} %get-tuple-element.472), channel_id=1, replica_groups=mesh['src'=8,'tgt'=16] {'src'}, use_global_device_ids=true, to_apply=%region_18.19 | all-reduce | flops 2048 | bytes 16384 | tf_op jit(solution)/shard_map/pmax | solution.py:20
  382.7 12.8 %psum.65 = f32[2048]{0:T(1024)S(1)} all-reduce(f32[2048]{0:T(1024)S(1)} %exponential_multiply_fusion.6), channel_id=1, replica_groups=mesh['src'=8,'tgt'=16] {'src'}, use_global_device_ids=true, to_apply=%region_19.20 | all-reduce | flops 2048 | bytes 16384 | tf_op jit(solution)/shard_map/psum | solution.py:21
  395.6 39.1 %while.96 = (s32[]{:T(128)}, f32[2048]{0:T(1024)S(1)}, f32[2048]{0:T(1024)S(1)}, f32[4,512]{1,0:T(4,128)S(1)}, f32[4,512]{1,0:T(4,128)S(1)}, /*index=5*/pred[4,2...) while((s32[]{:T(128)}, f32[2048]{0:T(1024)S(1)}, ...), condition=%wide.region_27.28_spmd.clone, body=%wide.region_22.27_spmd.clone.sunk | while | flops 302001152 | bytes 9287916 | solution.py:106
  395.8 3.8 fusion.150
  399.6 5.6 fusion.151
  405.6 3.8 fusion.150
  409.4 5.6 fusion.151
  415.4 3.8 fusion.150
  419.2 5.6 fusion.151
  425.1 3.8 fusion.150
  428.9 5.6 fusion.151
  434.7 30.7 %pmax.68 = f32[2048]{0:T(1024)S(1)} all-reduce(f32[2048]{0:T(1024)S(1)} %bitcast.459), channel_id=1, replica_groups=mesh['src'=8,'tgt'=16] {'tgt'}, use_global_device_ids=true, to_apply=%region_30.31 | all-reduce | flops 2048 | bytes 16384 | tf_op jit(solution)/shard_map/pmax | solution.py:14
  465.5 29.0 %psum.68 = f32[2048]{0:T(1024)S(1)} all-reduce(f32[2048]{0:T(1024)S(1)} %exponential_multiply_fusion.3), channel_id=1, replica_groups=mesh['src'=8,'tgt'=16] {'tgt'}, use_global_device_ids=true, to_apply=%region_31.32 | all-reduce | flops 2048 | bytes 16384 | tf_op jit(solution)/shard_map/psum | solution.py:15
  494.5 26.9 %pmax.67 = f32[2048]{0:T(1024)S(1)} all-reduce(f32[2048]{0:T(1024)S(1)} %get-tuple-element.476), channel_id=1, replica_groups=mesh['src'=8,'tgt'=16] {'src'}, use_global_device_ids=true, to_apply=%region_28.29 | all-reduce | flops 2048 | bytes 16384 | tf_op jit(solution)/shard_map/pmax | solution.py:20
  521.4 12.7 %psum.67 = f32[2048]{0:T(1024)S(1)} all-reduce(f32[2048]{0:T(1024)S(1)} %exponential_multiply_fusion.4), channel_id=1, replica_groups=mesh['src'=8,'tgt'=16] {'src'}, use_global_device_ids=true, to_apply=%region_29.30 | all-reduce | flops 2048 | bytes 16384 | tf_op jit(solution)/shard_map/psum | solution.py:21
  534.1 39.2 %while.97 = (s32[]{:T(128)}, f32[2048]{0:T(1024)S(1)}, f32[2048]{0:T(1024)S(1)}, f32[4,512]{1,0:T(4,128)S(1)}, f32[4,512]{1,0:T(4,128)S(1)}, /*index=5*/pred[4,2...) while((s32[]{:T(128)}, f32[2048]{0:T(1024)S(1)}, ...), condition=%wide.region_37.38_spmd.clone, body=%wide.region_32.37_spmd.clone.sunk | while | flops 302001152 | bytes 9287916 | solution.py:106
  534.3 3.8 fusion.154
  538.2 5.6 fusion.155
  544.1 3.8 fusion.154
  548.0 5.6 fusion.155
  553.9 3.8 fusion.154
  557.8 5.6 fusion.155
  563.7 3.8 fusion.154
  567.6 5.6 fusion.155
  573.4 12.7 %pmax.69 = f32[2048]{0:T(1024)S(1)} all-reduce(f32[2048]{0:T(1024)S(1)} %get-tuple-element.480), channel_id=1, replica_groups=mesh['src'=8,'tgt'=16] {'src'}, use_global_device_ids=true, to_apply=%region_38.39 | all-reduce | flops 2048 | bytes 16384 | tf_op jit(solution)/shard_map/pmax | solution.py:20
  586.0 12.7 %psum.69 = f32[2048]{0:T(1024)S(1)} all-reduce(f32[2048]{0:T(1024)S(1)} %exponential_multiply_fusion.2), channel_id=1, replica_groups=mesh['src'=8,'tgt'=16] {'src'}, use_global_device_ids=true, to_apply=%region_39.40 | all-reduce | flops 2048 | bytes 16384 | tf_op jit(solution)/shard_map/psum | solution.py:21
  598.8 9.7 %while.92 = (s32[]{:T(128)}, f32[4,512]{1,0:T(4,128)S(1)}, f32[4,512]{1,0:T(4,128)S(1)}, pred[4,2,2048]{2,1,0:T(4,128)(4,1)S(1)}, f32[8,256]{1,0:T(8,128)S(1)}, ...) while((s32[]{:T(128)}, f32[4,512]{1,0:T(4,128)S(1)}, ...), condition=%wide.region_43.44_spmd.clone, body=%wide.region_40.43_spmd.clone.sunk | while | flops 281019392 | bytes 9136305 | solution.py:130
  608.5 57.2 %all-reduce.1 = (f32[2048]{0:T(1024)S(1)}, f32[2048]{0:T(1024)S(1)}) all-reduce(f32[2048]{0:T(1024)S(1)} %bitcast.461, f32[2048]{0:T(1024)S(1)} %bitcast.463), channel_id=1, replica_groups=mesh['src'=8,'tgt'=16] {'tgt'}, use_global_device_ids=true, to_apply=%region_44.45 | all-reduce | flops 4096 | bytes 32768 | tf_op jit(solution)/shard_map/pmax | solution.py:14
  665.8 56.1 %all-reduce = (f32[4,512]{1,0:T(4,128)S(1)}, f32[2048]{0:T(1024)S(1)}) all-reduce(f32[4,512]{1,0:T(4,128)S(1)} %reshape.196, f32[2048]{0:T(1024)S(1)} %get-tuple-element.969), channel_id=1, replica_groups=mesh['src'=8,'tgt'=16] {'tgt'}, use_global_device_ids=true, to_apply=%region_45.46 | all-reduce | flops 4096 | bytes 32768 | tf_op jit(solution)/shard_map/psum | solution.py:15
  721.9 43.2 %while.93 = (s32[]{:T(128)}, f32[4,512,128]{2,1,0:T(8,128)}, pred[4,2,2048]{2,1,0:T(4,128)(4,1)S(1)}, f32[8,256]{1,0:T(8,128)S(1)}, f32[2048]{0:T(1024)S(1)}, /*...) while((s32[]{:T(128)}, f32[4,512,128]{2,1,0:T(8,128)}, ...), condition=%wide.region_47.48_spmd.clone, body=%wide.region_46.47_spmd.clone.sunk | while | flops 1888552960 | bytes 12532405 | solution.py:143
  725.0 7.7 fusion.140
  735.8 7.7 fusion.140
  746.6 7.7 fusion.140
  757.4 7.8 fusion.140
  766.6 92.2 %reduce-scatter.2.cloned.1.call-done = f32[8,16,128]{2,1,0:T(8,128)} async-done(((f32[8,256,128]{2,1,0:T(8,128)}), f32[8,16,128]{2,1,0:T(8,128)}) %reduce-scatter.2.cloned.1.call-update) | async-done | bytes 65552 | tf_op jit(solution)/shard_map/reduce_scatter | solution.py:146
  (359 shorter events, 33.9 us)
Async XLA Ops:
  7.2 71.8 %copy-start.3 = (s32[8]{0:T(128)S(1)}, s32[8]{0:T(128)}, u32[]{:S(2)}) copy-start(s32[8]{0:T(128)} %param.27) | copy-start | bytes 100
  7.2 72.0 %copy-start.1 = (bf16[8,16]{1,0:T(8,128)(2,1)S(1)}, bf16[8,16]{1,0:T(8,128)(2,1)}, u32[]{:S(2)}) copy-start(bf16[8,16]{1,0:T(8,128)(2,1)} %param.25) | copy-start | bytes 772
  7.2 88.2 %copy-start.2 = (bf16[8,32]{1,0:T(8,128)(2,1)S(1)}, bf16[8,32]{1,0:T(8,128)(2,1)}, u32[]{:S(2)}) copy-start(bf16[8,32]{1,0:T(8,128)(2,1)} %param.26) | copy-start | bytes 1540
  7.2 110.7 %copy-start = (s32[8]{0:T(128)S(1)}, s32[8]{0:T(128)}, u32[]{:S(2)}) copy-start(s32[8]{0:T(128)} %param.28) | copy-start | bytes 100
  7.2 851.6 %reduce-scatter.2.cloned.1.call-start = ((), (), s32[]{:S(2)}) async-start(), calls=%async_computation.1 | async-start | bytes 1114112 | tf_op jit(solution)/shard_map/reduce_scatter | solution.py:146
Sparse Core Ops, SparseCore 0:
  765.3 93.4 reduce-scatter.1
where the time goes:
time: 867 us; the launch traced here: 866 us
  blocking collectives  545 us (63%)
  matrix products  108 us (12%)
  other arithmetic  98.3 us (11%)
  waiting for transfers between devices  92.2 us (11%)
  between operations  14.8 us (2%)
    pmax x4, blocking collectives, row_lse(): top = lax.pmax(peak, 'tgt')  150 us
    psum x4, blocking collectives, row_lse(): whole = (top, lax.psum(total * jnp.exp(peak - top), 'tgt'))  143 us
    pmax x4, blocking collectives, col_lse(): top = lax.pmax(peak, 'src')  92.5 us
    reduce_scatter x1, waiting for transfers between devices, on_device(): lax.psum_scatter(moved.reshape(sb, blk, width), 'tgt', scatter_dimension=...  92.2 us
    reduce_sum x16, other arithmetic, visit(): return ((top, colsum), (peak, jnp.sum(weights, axis=1)))  90 us
    dot_general x24, matrix products, tile(): lax.dot_general(x, y_flat, (((1,), (1,)), ((), ())), preferred_element_ty...  77 us
    psum x4, blocking collectives, col_lse(): whole = (top, lax.psum(total * jnp.exp(peak - top), 'src'))  50.9 us
    dot_general x4, matrix products, project(): jnp.dot(weights, y_wide, precision=lax.Precision.HIGHEST)  30.9 us
  transfers between devices with their start and end apart: 1, of which 1 were waited for; matrix products, arithmetic and copies ran while one was open for 0% of the time, Pallas kernels for 0%

commit v1 on v0

v1 whole, which is shorter than its diff:
```python
import math

import jax
import jax.numpy as jnp
from jax import lax
from jax.experimental import pallas as pl
from jax.experimental.pallas import tpu as pltpu
from jax.sharding import PartitionSpec as P

ITERS = 4
EPSILON = 0.1
NEG = -1e30
SCALE = math.log2(math.e) / EPSILON
MESH = pl.DeviceIdType.MESH

NT, NS = 16, 8
PTS = 2048
TILES = 16
FAR_T = sorted(range(1, NT), key=lambda d: -(min(d // 4, 4 - d // 4) + min(d % 4, 4 - d % 4)))
FAR_S = sorted(range(1, NS), key=lambda d: -(2 * min(d // 2, 4 - d // 2) + d % 2))


def iota(shape, dim):
    return lax.broadcasted_iota(jnp.int32, shape, dim)


def tree(op, parts):
    parts = list(parts)
    while len(parts) > 1:
        parts = [op(parts[i], parts[i + 1]) if i + 1 < len(parts) else parts[i] for i in range(0, len(parts), 2)]
    return parts[0]


def fold(op, block):
    return tree(op, [block[8 * i : 8 * i + 8, :] for i in range(block.shape[0] // 8)])


def to_lanes(block):
    n = block.shape[1]
    put = (iota((n, 8 * n), 1) % n == iota((n, 8 * n), 0)).astype(jnp.bfloat16)
    wide = jnp.dot(block, put, preferred_element_type=jnp.float32)
    own = iota((8, 8 * n), 1) // n == iota((8, 8 * n), 0)
    return jnp.sum(jnp.where(own, wide, 0.0), axis=0, keepdims=True)


def half_norm(points):
    wide = points.astype(jnp.float32)
    square = wide * wide
    high = square.astype(jnp.bfloat16)
    low = (square - high.astype(jnp.float32)).astype(jnp.bfloat16)
    ones = jnp.ones((8, 128), jnp.bfloat16)
    dims = (((1,), (1,)), ((), ()))
    total = lax.dot_general(ones, high, dims, preferred_element_type=jnp.float32) + lax.dot_general(
        ones, low, dims, preferred_element_type=jnp.float32
    )
    return 0.5 * total[0:1, :]


def kernel(
    scnt, tcnt, keep, x_in, y_in, a_in, b_in, f_in, g_in, img_out, f_out, g_out,
    xs, ys, sp, tp, ytr, cmat, rmat, vbuf, fb, gb, pn, pt, whi, wlo, fl, gl,
    rsend, rrecv, csend, crecv, msg, mrecv,
    xsem, spsem, ysem, tpsem, rsem, csem, msem,
):
    src = lax.axis_index("src")
    tgt = lax.axis_index("tgt")
    sz, sc = lax.div(src, 2), lax.rem(src, 2)
    tx, ty = lax.div(tgt, 4), lax.rem(tgt, 4)

    def tpeer(d):
        return lax.rem(tx + d // 4, 4) * 4 + lax.rem(ty + d % 4, 4)

    def speer(d):
        return lax.rem(sz + d // 2, 4) * 2 + lax.rem(sc + d % 2, 2)

    barrier = pltpu.get_barrier_semaphore()
    for d in FAR_T:
        pl.semaphore_signal(barrier, inc=1, device_id={"tgt": tpeer(d)}, device_id_type=MESH)
    for d in FAR_S:
        pl.semaphore_signal(barrier, inc=1, device_id={"src": speer(d)}, device_id_type=MESH)

    def push(source, dest, sem, device):
        pltpu.make_async_remote_copy(
            src_ref=source, dst_ref=dest, send_sem=sem.at[0], recv_sem=sem.at[1], device_id=device, device_id_type=MESH
        ).start()

    def done(ref, sem):
        pltpu.make_async_copy(ref, ref, sem).wait()

    lane = iota((1, 128), 1)
    xs[pl.ds(tgt, 1)] = x_in[...].reshape(1, 128, 128)
    ys[pl.ds(src * 2, 2)] = y_in[...].reshape(2, 128, 128)
    fl[...] = jnp.zeros((8, 128), jnp.float32)
    gl[...] = jnp.zeros((2, 8, 128), jnp.float32)
    fl[0:1, :] = to_lanes(f_in[...])
    fl[1:2, :] = jnp.log2(to_lanes(a_in[...]))
    fl[2:3, :] = half_norm(x_in[...])
    tgt_rows = (to_lanes(g_in[...]), jnp.log2(to_lanes(b_in[...])), half_norm(y_in[...].reshape(256, 128)))
    for r, row in enumerate(tgt_rows):
        for h in range(2):
            gl[h, r : r + 1, :] = row[:, 128 * h : 128 * h + 128]
    sp[pl.ds(tgt, 1)] = fl[...].reshape(1, 8, 128)
    tp[pl.ds(src * 2, 2)] = gl[...]

    pl.semaphore_wait(barrier, len(FAR_T) + len(FAR_S))
    for d in FAR_T:
        push(x_in, xs.at[tgt], xsem, {"tgt": tpeer(d)})
    for d in FAR_S:
        push(y_in, ys.at[pl.ds(src * 2, 2)], ysem, {"src": speer(d)})
    for d in FAR_T:
        push(fl, sp.at[tgt], spsem, {"tgt": tpeer(d)})
    for d in FAR_S:
        push(gl, tp.at[pl.ds(src * 2, 2)], tpsem, {"src": speer(d)})

    for p in range(8):
        for par in range(2):
            row = jnp.zeros((1, 128), jnp.float32)
            for q in range(4):
                pen = jnp.where(keep[p, par * 4 + q] > 0, 0.0, NEG)
                row = jnp.where(lane // 32 == q, pen, row)
            pn[par, pl.ds(16 * p, 16), :] = jnp.broadcast_to(row, (16, 128))
    for q in range(8):
        row = jnp.zeros((1, 128), jnp.float32)
        for p in range(8):
            pen = jnp.where(keep[p, q] > 0, 0.0, NEG)
            row = jnp.where(lane // 16 == p, pen, row)
        pt[pl.ds(32 * q, 32), :] = jnp.broadcast_to(row, (32, 128))
    r16, l16 = iota((16, 128), 0), iota((16, 128), 1)
    sdead = jnp.zeros((16, 128), jnp.float32)
    tdead = jnp.zeros((16, 128), jnp.float32)
    for p in range(8):
        sdead = jnp.where((l16 // 16 == p) & (r16 * 16 + l16 % 16 >= scnt[p]), NEG, sdead)
        tdead = jnp.where(((r16 % 2) * 4 + l16 // 32 == p) & ((r16 // 2) * 32 + l16 % 32 >= tcnt[p]), NEG, tdead)
    eye = iota((128, 128), 0) == iota((128, 128), 1)

    def spread(rows, dest):
        for t in range(TILES):
            diag = jnp.where(eye, jnp.broadcast_to(rows[t : t + 1, :], (128, 128)), 0.0)
            column = jnp.sum(diag, axis=1, keepdims=True)
            dest[pl.ds(128 * t, 128), :] = jnp.broadcast_to(column, (128, 128))

    def score(mat, points, others, penalty, span):
        def pair(c, carry):
            two = points[pl.ds(2 * c, 2)].reshape(256, 128)
            for r in range(8):
                part = others[2 * r : 2 * r + 2].reshape(256, 128)
                prod = lax.dot_general(part, two, (((1,), (1,)), ((), ())), preferred_element_type=jnp.float32)
                for h in range(2):
                    mat[2 * c + h, pl.ds(256 * r, 256), :] = SCALE * prod[:, 128 * h : 128 * h + 128] + penalty(h)
            return carry

        lax.fori_loop(0, TILES // 2, pair, 0)

    def weigh(mat, c, col, slot):
        tops = []
        for r in range(16):
            v = mat[c, pl.ds(128 * r, 128), :] + col[pl.ds(128 * r, 128), :]
            vbuf[slot, pl.ds(128 * r, 128), :] = v
            tops.append(fold(jnp.maximum, v))
        return jnp.max(tree(jnp.maximum, tops), axis=0, keepdims=True)

    def lse(mat, col, out):
        def step(i, carry):
            for h in range(2):
                c = 2 * i + h
                top = weigh(mat, c, col, h)
                sums = []
                for r in range(16):
                    sums.append(fold(jnp.add, jnp.exp2(vbuf[h, pl.ds(128 * r, 128), :] - top)))
                total = jnp.sum(tree(jnp.add, sums), axis=0, keepdims=True)
                out[pl.ds(c, 1), :] = top + jnp.log2(total)
            return carry

        lax.fori_loop(0, TILES // 2, step, 0)

    def merge(ref, k):
        top = tree(jnp.maximum, [ref[k, i] for i in range(ref.shape[1])])
        total = tree(jnp.add, [jnp.exp2(ref[k, i] - top) for i in range(ref.shape[1])])
        return top + jnp.log2(total)

    done(ys.at[pl.ds(0, 14)], ysem.at[1])
    done(tp.at[pl.ds(0, 14)], tpsem.at[1])
    done(xs.at[pl.ds(0, 15)], xsem.at[1])
    done(sp.at[pl.ds(0, 15)], spsem.at[1])

    def rows_of(ref, r):
        return jnp.concatenate([ref[t, r : r + 1, :] for t in range(TILES)], axis=0)

    f, la, xh = rows_of(sp, 0), rows_of(sp, 1), rows_of(sp, 2)
    g, lb, yh = rows_of(tp, 0), rows_of(tp, 1), rows_of(tp, 2)
    la = la + sdead
    lb = lb + tdead
    spread(lb + SCALE * (g - yh), gb)
    spread(la + SCALE * (f - xh), fb)
    score(rmat, xs, ys, lambda h: pt[...], 256)

    def send_rows(k):
        rrecv[k, pl.ds(tgt, 1)] = rsend[k].reshape(1, 16, 128)
        for d in FAR_T:
            push(rsend.at[k], rrecv.at[k, tgt], rsem.at[k], {"tgt": tpeer(d)})

    def send_cols(k):
        crecv[k, pl.ds(src, 1)] = csend[k].reshape(1, 16, 128)
        for d in FAR_S:
            push(csend.at[k], crecv.at[k, src], csem.at[k], {"src": speer(d)})

    def take_rows(k, f):
        done(rrecv.at[k, pl.ds(0, 15)], rsem.at[k, 1])
        f = 0.5 * (f + (xh - merge(rrecv, k) * (1.0 / SCALE)))
        return f

    def take_cols(k, g):
        done(crecv.at[k, pl.ds(0, 7)], csem.at[k, 1])
        g = 0.5 * (g + (yh - merge(crecv, k) * (1.0 / SCALE)))
        return g

    lse(rmat, gb, rsend.at[0])
    send_rows(0)
    score(cmat, ys, xs, lambda h: jnp.concatenate([pn[h], pn[h]], axis=0), 256)
    for t in range(TILES):
        ytr[:, pl.ds(128 * t, 128)] = jnp.transpose(ys[t].astype(jnp.float32)).astype(jnp.bfloat16)
    lse(cmat, fb, csend.at[0])
    send_cols(0)
    for k in range(1, ITERS):
        if k % 2:
            f = take_rows(k - 1, f)
            spread(la + SCALE * (f - xh), fb)
            lse(cmat, fb, csend.at[k])
            send_cols(k)
            g = take_cols(k - 1, g)
            spread(lb + SCALE * (g - yh), gb)
            lse(rmat, gb, rsend.at[k])
            send_rows(k)
        else:
            g = take_cols(k - 1, g)
            spread(lb + SCALE * (g - yh), gb)
            lse(rmat, gb, rsend.at[k])
            send_rows(k)
            f = take_rows(k - 1, f)
            spread(la + SCALE * (f - xh), fb)
            lse(cmat, fb, csend.at[k])
            send_cols(k)
    g = take_cols(ITERS - 1, g)
    spread(lb + SCALE * (g - yh), gb)

    def project(i, carry):
        d = 15 - i
        c = lax.rem(tx + lax.div(d, 4), 4) * 4 + lax.rem(ty + lax.rem(d, 4), 4)
        top = weigh(rmat, c, gb, 0)
        sums = []
        for r in range(16):
            w = jnp.exp2(vbuf[0, pl.ds(128 * r, 128), :] - top)
            high = w.astype(jnp.bfloat16)
            whi[pl.ds(128 * r, 128), :] = high
            wlo[pl.ds(128 * r, 128), :] = (w - high.astype(jnp.float32)).astype(jnp.bfloat16)
            sums.append(fold(jnp.add, w))
        total = jnp.sum(tree(jnp.add, sums), axis=0, keepdims=True)
        moved = jnp.dot(ytr[...], whi[...], preferred_element_type=jnp.float32) + jnp.dot(
            ytr[...], wlo[...], preferred_element_type=jnp.float32
        )
        msg[d, 0:128, :] = moved
        r8 = iota((8, 128), 0)
        msg[d, 128:136, :] = jnp.where(r8 == 0, top, jnp.where(r8 == 1, total, 0.0))

        @pl.when(d > 0)
        def _():
            push(msg.at[d], mrecv.at[d], msem, {"tgt": c})

        return carry

    lax.fori_loop(0, 16, project, 0)
    f = take_rows(ITERS - 1, f)
    fb[0:16, :] = f
    f_out[...] = fb[pl.ds(tgt, 1), :]
    gb[0:16, :] = g
    g_out[...] = gb[pl.ds(src * 2, 2), :]
    mrecv[0] = msg[0]
    done(mrecv.at[pl.ds(1, 15)], msem.at[1])
    tops = [mrecv[d, 128:129, :] for d in range(16)]
    top = tree(jnp.maximum, tops)
    scales = [jnp.exp2(t - top) for t in tops]
    total = tree(jnp.add, [scales[d] * mrecv[d, 129:130, :] for d in range(16)])
    inv = 1.0 / total
    moved = scales[0] * mrecv[0, 0:128, :]
    for d in range(1, 16):
        moved = moved + scales[d] * mrecv[d, 0:128, :]
    img_out[...] = jnp.transpose(moved * inv)

    done(xs.at[pl.ds(0, 15)], xsem.at[0])
    done(sp.at[pl.ds(0, 15)], spsem.at[0])
    done(ys.at[pl.ds(0, 14)], ysem.at[0])
    done(tp.at[pl.ds(0, 14)], tpsem.at[0])
    for k in range(ITERS):
        done(rrecv.at[k, pl.ds(0, 15)], rsem.at[k, 0])
        done(crecv.at[k, pl.ds(0, 7)], csem.at[k, 0])
    done(mrecv.at[pl.ds(1, 15)], msem.at[0])


def on_device(src_points, tgt_points, src_mass, tgt_mass, src_potential, tgt_potential, src_counts, tgt_counts, keep):
    f32, bf16 = jnp.float32, jnp.bfloat16
    vmem = pl.BlockSpec(memory_space=pltpu.VMEM)
    smem = pl.BlockSpec(memory_space=pltpu.SMEM)
    dma = pltpu.SemaphoreType.DMA
    images, f, g = pl.pallas_call(
        kernel,
        out_shape=(
            jax.ShapeDtypeStruct((128, 128), f32),
            jax.ShapeDtypeStruct((1, 128), f32),
            jax.ShapeDtypeStruct((2, 128), f32),
        ),
        in_specs=[smem] * 3 + [vmem] * 6,
        out_specs=(vmem, vmem, vmem),
        scratch_shapes=[
            pltpu.VMEM((16, 128, 128), bf16),
            pltpu.VMEM((16, 128, 128), bf16),
            pltpu.VMEM((16, 8, 128), f32),
            pltpu.VMEM((16, 8, 128), f32),
            pltpu.VMEM((128, PTS), bf16),
            pltpu.VMEM((16, PTS, 128), f32),
            pltpu.VMEM((16, PTS, 128), f32),
            pltpu.VMEM((2, PTS, 128), f32),
            pltpu.VMEM((PTS, 128), f32),
            pltpu.VMEM((PTS, 128), f32),
            pltpu.VMEM((2, 128, 128), f32),
            pltpu.VMEM((256, 128), f32),
            pltpu.VMEM((PTS, 128), bf16),
            pltpu.VMEM((PTS, 128), bf16),
            pltpu.VMEM((8, 128), f32),
            pltpu.VMEM((2, 8, 128), f32),
            pltpu.VMEM((ITERS, 16, 128), f32),
            pltpu.VMEM((ITERS, 16, 16, 128), f32),
            pltpu.VMEM((ITERS, 16, 128), f32),
            pltpu.VMEM((ITERS, 8, 16, 128), f32),
            pltpu.VMEM((16, 136, 128), f32),
            pltpu.VMEM((16, 136, 128), f32),
            dma((2,)),
            dma((2,)),
            dma((2,)),
            dma((2,)),
            dma((ITERS, 2)),
            dma((ITERS, 2)),
            dma((2,)),
        ],
        compiler_params=pltpu.CompilerParams(
            collective_id=0, has_side_effects=True, vmem_limit_bytes=60 * 1024 * 1024
        ),
        name="sinkhorn",
    )(
        src_counts,
        tgt_counts,
        keep,
        src_points.reshape(128, 128),
        tgt_points.reshape(2, 128, 128),
        src_mass,
        tgt_mass,
        src_potential,
        tgt_potential,
    )
    return images.reshape(8, 16, 128), f.reshape(8, 16), g.reshape(8, 32)


def solution(mesh):
    return jax.shard_map(
        on_device,
        mesh=mesh,
        in_specs=(
            P("src", "tgt", None),
            P("tgt", "src", None),
            P("src", "tgt"),
            P("tgt", "src"),
            P("src", "tgt"),
            P("tgt", "src"),
            P("src"),
            P("tgt"),
            P("src", "tgt"),
        ),
        out_specs=(P("src", "tgt", None), P("src", "tgt"), P("tgt", "src")),
        check_vma=False,
    )
```

time: 867 us -> 86.9 us (0.10)
  blocking collectives: 545 us -> 0 us
  matrix products: 108 us -> 0 us
  other arithmetic: 98.3 us -> 0.66 us
  waiting for transfers between devices: 92.2 us -> 0 us
  Pallas kernels: 0 us -> 80.7 us
  between operations: 14.8 us -> 0.65 us
    pmax x8 -> x0, blocking collectives: 243 us -> none  [the longest x4 150 us: row_lse(): top = lax.pmax(peak, 'tgt')]
    psum x8 -> x0, blocking collectives: 194 us -> none  [the longest x4 143 us: row_lse(): whole = (top, lax.psum(total * jnp.exp(peak - top), 'tgt'))]
    all_gather x6 -> x0, blocking collectives: 108 us -> none  [the longest x1 22.4 us: on_device(): lax.all_gather(tgt_potential, 'src', axis=1, tiled=True)]
    dot_general x28 -> x0, matrix products: 108 us -> none  [the longest x24 77 us: tile(): lax.dot_general(x, y_flat, (((1,), (1,)), ((), ())), preferred_element_ty...]
    reduce_sum x22 -> x0, other arithmetic: 94.1 us -> none  [the longest x16 90 us: visit(): return ((top, colsum), (peak, jnp.sum(weights, axis=1)))]
    reduce_scatter x1 -> x0, waiting for transfers between devices: 92.2 us -> none  [on_device(): lax.psum_scatter(moved.reshape(sb, blk, width), 'tgt', scatter_dimension=...]
    pallas_call x0 -> x1, Pallas kernels: none -> 80.7 us  [on_device(): pl.pallas_call(kernel, out_shape=(jax.ShapeDtypeStruct((128, 128), f32),...]
  transfers between devices with their start and end apart: 1 -> 0, of which waited for: 1 -> 0; matrix products, arithmetic and copies ran while one was open for 0% -> 0% of each run, Pallas kernels for 0% -> 0%
where the time goes in v1:
time: 86.9 us; the launch traced here: 86 us
  Pallas kernels  80.7 us (93%)
  local copies, waits for them, and re-layouts  4.04 us (5%)
    pallas_call x1, Pallas kernels, on_device(): pl.pallas_call(kernel, out_shape=(jax.ShapeDtypeStruct((128, 128), f32),...  80.7 us
    unnamed x5, local copies, waits for them, and re-layouts  2.18 us

profile of v1, /device:TPU:1, one launch (start us, length us, event | category | flops | bytes accessed | tf_op | source)
XLA Modules:
  0.0 86.0 jit_solution(11358061733004630237)
XLA Ops:
  0.6 80.7 %sinkhorn.1 = (f32[128,128]{1,0:T(8,128)}, f32[1,128]{1,0:T(1,128)}, f32[2,128]{1,0:T(2,128)}) custom-call(s32[8]{0:T(128)} %scnt.1, s32[8]{0:T(128)} %tcnt.1, s32[8,8]{1,0:T(8,128)} %keep.1, bf16[128,128]{1,0:T(8,128)(2,1)} %bitcast.5, bf16[2,128,128]{2,1,0:T(8,128)(2,1)} %bitcast.3, bf16[8,16]{1,0:T(8,128)(2,1)} %a_in.1, bf16[8,32]{1,0:T(8,128)(2,1)} %b_in.1, ...), custom_call_target="tpu_custom_call" | custom-call | tf_op jit(solution)/shard_map/sinkhorn/pallas_call | solution.py:304
  81.3 0.0 copy-start.1
  81.3 0.5 broadcast.3
  81.8 0.1 copy-done.1
  81.9 0.7 reduce.3
  82.6 0.7 reshape.24
  83.3 0.0 copy-start
  83.3 0.6 copy-done
  83.9 0.7 reshape.25
  84.6 1.5 %copy.13 = f32[8,16,128]{2,1,0:T(8,128)} copy(f32[8,16,128]{2,1,0:T(8,128)} %bitcast.4) | data formatting | bytes 131072
Async XLA Ops:
  81.3 0.6 copy-start.1
  83.3 0.6 copy-start

commit v2 on v1

--- a/solution.py
+++ b/solution.py
@@ -16,7 +16,9 @@
 NT, NS = 16, 8
 PTS = 2048
 TILES = 16
+WIDE = 4
 FAR_T = sorted(range(1, NT), key=lambda d: -(min(d // 4, 4 - d // 4) + min(d % 4, 4 - d % 4)))
+LINE = (1, 3, 2)
 FAR_S = sorted(range(1, NS), key=lambda d: -(2 * min(d // 2, 4 - d // 2) + d % 2))
 
 
@@ -41,6 +43,21 @@
     wide = jnp.dot(block, put, preferred_element_type=jnp.float32)
     own = iota((8, 8 * n), 1) // n == iota((8, 8 * n), 0)
     return jnp.sum(jnp.where(own, wide, 0.0), axis=0, keepdims=True)
+
+
+def from_lanes(rows, n):
+    per = 128 // n
+    home, lane = iota((8, 128), 0), iota((8, 128), 1)
+    wide = jnp.zeros((8, 128), jnp.float32)
+    for h in range(rows.shape[0]):
+        wide = jnp.where(home == h * per + lane // n, jnp.broadcast_to(rows[h : h + 1, :], (8, 128)), wide)
+    put = (iota((128, n), 0) % n == iota((128, n), 1)).astype(jnp.bfloat16)
+    high = wide.astype(jnp.bfloat16)
+    rest = wide - high.astype(jnp.float32)
+    mid = rest.astype(jnp.bfloat16)
+    low = (rest - mid.astype(jnp.float32)).astype(jnp.bfloat16)
+    parts = [jnp.dot(part, put, preferred_element_type=jnp.float32) for part in (high, mid, low)]
+    return parts[0] + parts[1] + parts[2]
 
 
 def half_norm(points):
@@ -103,10 +120,11 @@
     tp[pl.ds(src * 2, 2)] = gl[...]
 
     pl.semaphore_wait(barrier, len(FAR_T) + len(FAR_S))
-    for d in FAR_T:
-        push(x_in, xs.at[tgt], xsem, {"tgt": tpeer(d)})
-    for d in FAR_S:
-        push(y_in, ys.at[pl.ds(src * 2, 2)], ysem, {"src": speer(d)})
+    for i, n in enumerate(LINE):
+        push(x_in, xs.at[tgt], xsem.at[i], {"tgt": tpeer(4 * n)})
+        push(x_in, xs.at[tgt], xsem.at[3 + i], {"tgt": tpeer(n)})
+        push(y_in, ys.at[pl.ds(src * 2, 2)], ysem.at[i], {"src": speer(2 * n)})
+    push(y_in, ys.at[pl.ds(src * 2, 2)], ysem.at[3], {"src": speer(1)})
     for d in FAR_T:
         push(fl, sp.at[tgt], spsem, {"tgt": tpeer(d)})
     for d in FAR_S:
@@ -151,36 +169,49 @@
 
         lax.fori_loop(0, TILES // 2, pair, 0)
 
-    def weigh(mat, c, col, slot):
-        tops = []
-        for r in range(16):
-            v = mat[c, pl.ds(128 * r, 128), :] + col[pl.ds(128 * r, 128), :]
-            vbuf[slot, pl.ds(128 * r, 128), :] = v
-            tops.append(fold(jnp.maximum, v))
-        return jnp.max(tree(jnp.maximum, tops), axis=0, keepdims=True)
-
     def lse(mat, col, out):
         def step(i, carry):
-            for h in range(2):
-                c = 2 * i + h
-                top = weigh(mat, c, col, h)
-                sums = []
-                for r in range(16):
-                    sums.append(fold(jnp.add, jnp.exp2(vbuf[h, pl.ds(128 * r, 128), :] - top)))
-                total = jnp.sum(tree(jnp.add, sums), axis=0, keepdims=True)
-                out[pl.ds(c, 1), :] = top + jnp.log2(total)
+            tops, sums = [None] * WIDE, [None] * WIDE
+            for r in range(PTS // 128):
+                part = col[pl.ds(128 * r, 128), :]
+                for h in range(WIDE):
+                    v = mat[WIDE * i + h, pl.ds(128 * r, 128), :] + part
+                    vs = [v[8 * n : 8 * n + 8, :] for n in range(16)]
+                    top = tree(jnp.maximum, vs if r == 0 else vs + [tops[h]])
+                    total = tree(jnp.add, [jnp.exp2(u - top) for u in vs])
+                    sums[h] = total if r == 0 else sums[h] * jnp.exp2(tops[h] - top) + total
+                    tops[h] = top
+            for h in range(WIDE):
+                top = jnp.max(tops[h], axis=0, keepdims=True)
+                total = jnp.sum(sums[h] * jnp.exp2(tops[h] - top), axis=0, keepdims=True)
+                out[pl.ds(WIDE * i + h, 1), :] = top + jnp.log2(total)
             return carry
 
-        lax.fori_loop(0, TILES // 2, step, 0)
+        lax.fori_loop(0, TILES // WIDE, step, 0)
 
     def merge(ref, k):
         top = tree(jnp.maximum, [ref[k, i] for i in range(ref.shape[1])])
         total = tree(jnp.add, [jnp.exp2(ref[k, i] - top) for i in range(ref.shape[1])])
         return top + jnp.log2(total)
 
-    done(ys.at[pl.ds(0, 14)], ysem.at[1])
+    for i, n in enumerate(LINE):
+        got = tpeer(16 - 4 * n)
+        done(xs.at[got], xsem.at[i, 1])
+        for m in LINE:
+            half = xs.at[got, pl.ds(0, 64)]
+            push(half, half, xsem.at[6], {"tgt": tpeer(m)})
+        got = tpeer(4 - n)
+        done(xs.at[got], xsem.at[3 + i, 1])
+        for m in LINE:
+            half = xs.at[got, pl.ds(64, 64)]
+            push(half, half, xsem.at[6], {"tgt": tpeer(4 * m)})
+        piece = ys.at[pl.ds(speer(8 - 2 * n) * 2, 2)]
+        done(piece, ysem.at[i, 1])
+        push(piece, piece, ysem.at[4], {"src": speer(1)})
+    done(ys.at[pl.ds(0, 2)], ysem.at[3, 1])
+    done(ys.at[pl.ds(0, 6)], ysem.at[4, 1])
     done(tp.at[pl.ds(0, 14)], tpsem.at[1])
-    done(xs.at[pl.ds(0, 15)], xsem.at[1])
+    done(xs.at[pl.ds(0, 9)], xsem.at[6, 1])
     done(sp.at[pl.ds(0, 15)], spsem.at[1])
 
     def rows_of(ref, r):
@@ -217,8 +248,9 @@
     lse(rmat, gb, rsend.at[0])
     send_rows(0)
     score(cmat, ys, xs, lambda h: jnp.concatenate([pn[h], pn[h]], axis=0), 256)
+    ytr[128:144, :] = jnp.ones((16, PTS), jnp.bfloat16)
     for t in range(TILES):
-        ytr[:, pl.ds(128 * t, 128)] = jnp.transpose(ys[t].astype(jnp.float32)).astype(jnp.bfloat16)
+        ytr[0:128, pl.ds(128 * t, 128)] = jnp.transpose(ys[t].astype(jnp.float32)).astype(jnp.bfloat16)
     lse(cmat, fb, csend.at[0])
     send_cols(0)
     for k in range(1, ITERS):
@@ -244,36 +276,44 @@
     spread(lb + SCALE * (g - yh), gb)
 
     def project(i, carry):
-        d = 15 - i
-        c = lax.rem(tx + lax.div(d, 4), 4) * 4 + lax.rem(ty + lax.rem(d, 4), 4)
-        top = weigh(rmat, c, gb, 0)
-        sums = []
+        ds = [15 - 2 * i, 14 - 2 * i]
+        cs = [lax.rem(tx + lax.div(d, 4), 4) * 4 + lax.rem(ty + lax.rem(d, 4), 4) for d in ds]
+        tops = [[], []]
         for r in range(16):
-            w = jnp.exp2(vbuf[0, pl.ds(128 * r, 128), :] - top)
-            high = w.astype(jnp.bfloat16)
-            whi[pl.ds(128 * r, 128), :] = high
-            wlo[pl.ds(128 * r, 128), :] = (w - high.astype(jnp.float32)).astype(jnp.bfloat16)
-            sums.append(fold(jnp.add, w))
-        total = jnp.sum(tree(jnp.add, sums), axis=0, keepdims=True)
+            part = gb[pl.ds(128 * r, 128), :]
+            for h in range(2):
+                v = rmat[cs[h], pl.ds(128 * r, 128), :] + part
+                vbuf[h, pl.ds(128 * r, 128), :] = v
+                tops[h].append(fold(jnp.maximum, v))
+        tops = [jnp.max(tree(jnp.maximum, t), axis=0, keepdims=True) for t in tops]
+        for r in range(16):
+            for h in range(2):
+                w = jnp.exp2(vbuf[h, pl.ds(128 * r, 128), :] - tops[h])
+                high = w.astype(jnp.bfloat16)
+                whi[pl.ds(128 * r, 128), 128 * h : 128 * h + 128] = high
+                wlo[pl.ds(128 * r, 128), 128 * h : 128 * h + 128] = (w - high.astype(jnp.float32)).astype(jnp.bfloat16)
         moved = jnp.dot(ytr[...], whi[...], preferred_element_type=jnp.float32) + jnp.dot(
             ytr[...], wlo[...], preferred_element_type=jnp.float32
         )
-        msg[d, 0:128, :] = moved
         r8 = iota((8, 128), 0)
-        msg[d, 128:136, :] = jnp.where(r8 == 0, top, jnp.where(r8 == 1, total, 0.0))
-
-        @pl.when(d > 0)
+        for h in range(2):
+            msg[ds[h], 0:128, :] = moved[0:128, 128 * h : 128 * h + 128]
+            total = moved[128:136, 128 * h : 128 * h + 128]
+            msg[ds[h], 128:136, :] = jnp.where(r8 == 0, jnp.broadcast_to(tops[h], (8, 128)), total)
+        push(msg.at[ds[0]], mrecv.at[ds[0]], msem, {"tgt": cs[0]})
+
+        @pl.when(ds[1] > 0)
         def _():
-            push(msg.at[d], mrecv.at[d], msem, {"tgt": c})
+            push(msg.at[ds[1]], mrecv.at[ds[1]], msem, {"tgt": cs[1]})
 
         return carry
 
-    lax.fori_loop(0, 16, project, 0)
+    lax.fori_loop(0, 8, project, 0)
     f = take_rows(ITERS - 1, f)
     fb[0:16, :] = f
-    f_out[...] = fb[pl.ds(tgt, 1), :]
+    f_out[...] = from_lanes(fb[pl.ds(tgt, 1), :], 16)
     gb[0:16, :] = g
-    g_out[...] = gb[pl.ds(src * 2, 2), :]
+    g_out[...] = from_lanes(gb[pl.ds(src * 2, 2), :], 32)
     mrecv[0] = msg[0]
     done(mrecv.at[pl.ds(1, 15)], msem.at[1])
     tops = [mrecv[d, 128:129, :] for d in range(16)]
@@ -286,9 +326,13 @@
         moved = moved + scales[d] * mrecv[d, 0:128, :]
     img_out[...] = jnp.transpose(moved * inv)
 
-    done(xs.at[pl.ds(0, 15)], xsem.at[0])
+    for i in range(6):
+        done(xs.at[0], xsem.at[i, 0])
+    done(xs.at[pl.ds(0, 9)], xsem.at[6, 0])
+    for i in range(4):
+        done(ys.at[pl.ds(0, 2)], ysem.at[i, 0])
+    done(ys.at[pl.ds(0, 6)], ysem.at[4, 0])
     done(sp.at[pl.ds(0, 15)], spsem.at[0])
-    done(ys.at[pl.ds(0, 14)], ysem.at[0])
     done(tp.at[pl.ds(0, 14)], tpsem.at[0])
     for k in range(ITERS):
         done(rrecv.at[k, pl.ds(0, 15)], rsem.at[k, 0])
@@ -305,8 +349,8 @@
         kernel,
         out_shape=(
             jax.ShapeDtypeStruct((128, 128), f32),
-            jax.ShapeDtypeStruct((1, 128), f32),
-            jax.ShapeDtypeStruct((2, 128), f32),
+            jax.ShapeDtypeStruct((8, 16), f32),
+            jax.ShapeDtypeStruct((8, 32), f32),
         ),
         in_specs=[smem] * 3 + [vmem] * 6,
         out_specs=(vmem, vmem, vmem),
@@ -315,7 +359,7 @@
             pltpu.VMEM((16, 128, 128), bf16),
             pltpu.VMEM((16, 8, 128), f32),
             pltpu.VMEM((16, 8, 128), f32),
-            pltpu.VMEM((128, PTS), bf16),
+            pltpu.VMEM((144, PTS), bf16),
             pltpu.VMEM((16, PTS, 128), f32),
             pltpu.VMEM((16, PTS, 128), f32),
             pltpu.VMEM((2, PTS, 128), f32),
@@ -323,8 +367,8 @@
             pltpu.VMEM((PTS, 128), f32),
             pltpu.VMEM((2, 128, 128), f32),
             pltpu.VMEM((256, 128), f32),
-            pltpu.VMEM((PTS, 128), bf16),
-            pltpu.VMEM((PTS, 128), bf16),
+            pltpu.VMEM((PTS, 256), bf16),
+            pltpu.VMEM((PTS, 256), bf16),
             pltpu.VMEM((8, 128), f32),
             pltpu.VMEM((2, 8, 128), f32),
             pltpu.VMEM((ITERS, 16, 128), f32),
@@ -333,9 +377,9 @@
             pltpu.VMEM((ITERS, 8, 16, 128), f32),
             pltpu.VMEM((16, 136, 128), f32),
             pltpu.VMEM((16, 136, 128), f32),
+            dma((7, 2)),
             dma((2,)),
-            dma((2,)),
-            dma((2,)),
+            dma((5, 2)),
             dma((2,)),
             dma((ITERS, 2)),
             dma((ITERS, 2)),
@@ -356,7 +400,7 @@
         src_potential,
         tgt_potential,
     )
-    return images.reshape(8, 16, 128), f.reshape(8, 16), g.reshape(8, 32)
+    return images.reshape(8, 16, 128), f, g
 
 
 def solution(mesh):

time: 86.9 us -> 77.9 us (0.90)
  Pallas kernels: 80.7 us -> 74.3 us
  local copies, waits for them, and re-layouts: 4.04 us -> 2.74 us
    pallas_call x1, Pallas kernels: 80.7 us -> 74.3 us  [on_device(): pl.pallas_call(kernel, out_shape=(jax.ShapeDtypeStruct((128, 128), f32),...]
    reshape x2 -> x0, local copies, waits for them, and re-layouts: 1.34 us -> none  [on_device(): return (images.reshape(8, 16, 128), f.reshape(8, 16), g.reshape(8, 32))]
    unnamed x5 -> x7, local copies, waits for them, and re-layouts: 2.18 us -> 2.74 us
where the time goes in v2:
time: 77.9 us; the launch traced here: 77.7 us
  Pallas kernels  74.3 us (95%)
  local copies, waits for them, and re-layouts  2.74 us (4%)
    pallas_call x1, Pallas kernels, on_device(): pl.pallas_call(kernel, out_shape=(jax.ShapeDtypeStruct((128, 128), f32),...  74.3 us
    unnamed x7, local copies, waits for them, and re-layouts  2.74 us

profile of v2, /device:TPU:1, one launch (start us, length us, event | category | flops | bytes accessed | tf_op | source)
XLA Modules:
  0.0 77.7 jit_solution(7111709649318741511)
XLA Ops:
  0.6 74.3 %sinkhorn.1 = (f32[128,128]{1,0:T(8,128)}, f32[8,16]{1,0:T(8,128)}, f32[8,32]{1,0:T(8,128)}) custom-call(s32[8]{0:T(128)} %scnt.1, s32[8]{0:T(128)} %tcnt.1, s32[8,8]{1,0:T(8,128)} %keep.1, bf16[128,128]{1,0:T(8,128)(2,1)} %bitcast.5, bf16[2,128,128]{2,1,0:T(8,128)(2,1)} %bitcast.3, bf16[8,16]{1,0:T(8,128)(2,1)} %a_in.1, bf16[8,32]{1,0:T(8,128)(2,1)} %b_in.1, ...), custom_call_target="tpu_custom_call" | custom-call | tf_op jit(solution)/shard_map/sinkhorn/pallas_call | solution.py:348
  74.9 0.0 copy-start.1
  74.9 1.5 %copy.15 = f32[8,16,128]{2,1,0:T(8,128)} copy(f32[8,16,128]{2,1,0:T(8,128)} %bitcast.4) | data formatting | bytes 131072
  76.4 0.0 copy-done.1
  76.4 0.0 copy-start
  76.4 0.6 copy.16
  77.0 0.1 copy-done
  77.1 0.6 copy.17
Async XLA Ops:
  74.9 1.5 %copy-start.1 = (f32[8,16]{1,0:T(8,128)S(1)}, f32[8,16]{1,0:T(8,128)}, u32[]{:S(2)}) copy-start(f32[8,16]{1,0:T(8,128)} %get-tuple-element.13) | copy-start | bytes 1540
  76.4 0.7 copy-start

commit v3 on v2

v3 whole, which is shorter than its diff:
```python
import math

import jax
import jax.numpy as jnp
from jax import lax
from jax.experimental import pallas as pl
from jax.experimental.pallas import tpu as pltpu
from jax.sharding import PartitionSpec as P

ITERS = 4
EPSILON = 0.1
NEG = -1e30
SCALE = math.log2(math.e) / EPSILON
MESH = pl.DeviceIdType.MESH

NT, NS = 16, 8
PTS = 2048
TILES = 16
WIDE = 4
FAR_T = sorted(range(1, NT), key=lambda d: -(min(d // 4, 4 - d // 4) + min(d % 4, 4 - d % 4)))
LINE = (1, 3, 2)
FAR_S = sorted(range(1, NS), key=lambda d: -(2 * min(d // 2, 4 - d // 2) + d % 2))


def iota(shape, dim):
    return lax.broadcasted_iota(jnp.int32, shape, dim)


def tree(op, parts):
    parts = list(parts)
    while len(parts) > 1:
        parts = [op(parts[i], parts[i + 1]) if i + 1 < len(parts) else parts[i] for i in range(0, len(parts), 2)]
    return parts[0]


def fold(op, block):
    return tree(op, [block[8 * i : 8 * i + 8, :] for i in range(block.shape[0] // 8)])


def to_lanes(block):
    n = block.shape[1]
    put = (iota((n, 8 * n), 1) % n == iota((n, 8 * n), 0)).astype(jnp.bfloat16)
    wide = jnp.dot(block, put, preferred_element_type=jnp.float32)
    own = iota((8, 8 * n), 1) // n == iota((8, 8 * n), 0)
    return jnp.sum(jnp.where(own, wide, 0.0), axis=0, keepdims=True)


def thirds(wide):
    high = wide.astype(jnp.bfloat16)
    rest = wide - high.astype(jnp.float32)
    mid = rest.astype(jnp.bfloat16)
    return high, mid, (rest - mid.astype(jnp.float32)).astype(jnp.bfloat16)


def from_lanes(rows, n):
    per = 128 // n
    home, lane = iota((8, 128), 0), iota((8, 128), 1)
    wide = jnp.zeros((8, 128), jnp.float32)
    for h in range(rows.shape[0]):
        wide = jnp.where(home == h * per + lane // n, jnp.broadcast_to(rows[h : h + 1, :], (8, 128)), wide)
    put = (iota((128, n), 0) % n == iota((128, n), 1)).astype(jnp.bfloat16)
    parts = [jnp.dot(part, put, preferred_element_type=jnp.float32) for part in thirds(wide)]
    return parts[0] + parts[1] + parts[2]


def half_norm(points):
    wide = points.astype(jnp.float32)
    square = wide * wide
    high = square.astype(jnp.bfloat16)
    low = (square - high.astype(jnp.float32)).astype(jnp.bfloat16)
    ones = jnp.ones((8, 128), jnp.bfloat16)
    dims = (((1,), (1,)), ((), ()))
    total = lax.dot_general(ones, high, dims, preferred_element_type=jnp.float32) + lax.dot_general(
        ones, low, dims, preferred_element_type=jnp.float32
    )
    return 0.5 * total[0:1, :]


def kernel(
    scnt, tcnt, keep, x_in, y_in, a_in, b_in, f_in, g_in, img_out, f_out, g_out,
    xs, ys, sp, tp, ytr, cmat, rmat, vbuf, fb, gb, sel, pt, whi, wlo, fl, gl,
    rsend, rrecv, csend, crecv, msg, mrecv, stat, srecv,
    xsem, spsem, ysem, tpsem, rsem, csem, msem, ssem, kept,
):
    src = lax.axis_index("src")
    tgt = lax.axis_index("tgt")
    sz, sc = lax.div(src, 2), lax.rem(src, 2)
    tx, ty = lax.div(tgt, 4), lax.rem(tgt, 4)

    def tpeer(d):
        return lax.rem(tx + d // 4, 4) * 4 + lax.rem(ty + d % 4, 4)

    def speer(d):
        return lax.rem(sz + d // 2, 4) * 2 + lax.rem(sc + d % 2, 2)

    barrier = pltpu.get_barrier_semaphore()
    for n in LINE:
        pl.semaphore_signal(barrier, inc=1, device_id={"tgt": tpeer(4 * n)}, device_id_type=MESH)
        pl.semaphore_signal(barrier, inc=1, device_id={"tgt": tpeer(n)}, device_id_type=MESH)
        pl.semaphore_signal(barrier, inc=1, device_id={"src": speer(2 * n)}, device_id_type=MESH)
    pl.semaphore_signal(barrier, inc=1, device_id={"src": speer(1)}, device_id_type=MESH)

    def push(source, dest, sem, device):
        pltpu.make_async_remote_copy(
            src_ref=source, dst_ref=dest, send_sem=sem.at[0], recv_sem=sem.at[1], device_id=device, device_id_type=MESH
        ).start()

    def done(ref, sem):
        pltpu.make_async_copy(ref, ref, sem).wait()

    lane = iota((1, 128), 1)
    xs[pl.ds(tgt, 1)] = x_in[...].reshape(1, 128, 128)
    ys[pl.ds(src * 2, 2)] = y_in[...].reshape(2, 128, 128)
    fl[...] = jnp.zeros((8, 128), jnp.float32)
    gl[...] = jnp.zeros((2, 8, 128), jnp.float32)
    fl[0:1, :] = to_lanes(f_in[...])
    fl[1:2, :] = jnp.log2(to_lanes(a_in[...]))
    fl[2:3, :] = half_norm(x_in[...])
    tgt_rows = (to_lanes(g_in[...]), jnp.log2(to_lanes(b_in[...])), half_norm(y_in[...].reshape(256, 128)))
    for r, row in enumerate(tgt_rows):
        for h in range(2):
            gl[h, r : r + 1, :] = row[:, 128 * h : 128 * h + 128]
    sp[pl.ds(tgt, 1)] = fl[...].reshape(1, 8, 128)
    tp[pl.ds(src * 2, 2)] = gl[...]

    pl.semaphore_wait(barrier, 10)
    mine_y = pl.ds(src * 2, 2)
    for i, n in enumerate(LINE):
        push(fl, sp.at[tgt], spsem.at[i], {"tgt": tpeer(4 * n)})
        push(fl, sp.at[tgt], spsem.at[3], {"tgt": tpeer(n)})
        push(gl, tp.at[mine_y], tpsem.at[i], {"src": speer(2 * n)})
        push(x_in, xs.at[tgt], xsem.at[i], {"tgt": tpeer(4 * n)})
        push(x_in, xs.at[tgt], xsem.at[3 + i], {"tgt": tpeer(n)})
        push(y_in, ys.at[mine_y], ysem.at[i], {"src": speer(2 * n)})
    push(gl, tp.at[mine_y], tpsem.at[3], {"src": speer(1)})
    push(y_in, ys.at[mine_y], ysem.at[3], {"src": speer(1)})

    for q in range(8):
        row = jnp.zeros((1, 128), jnp.float32)
        for p in range(8):
            pen = jnp.where(keep[p, q] > 0, 0.0, NEG)
            row = jnp.where(lane // 16 == p, pen, row)
        pt[pl.ds(32 * q, 32), :] = jnp.broadcast_to(row, (32, 128))
    r16, l16 = iota((16, 128), 0), iota((16, 128), 1)
    sdead = jnp.zeros((16, 128), jnp.float32)
    tdead = jnp.zeros((16, 128), jnp.float32)
    for p in range(8):
        sdead = jnp.where((l16 // 16 == p) & (r16 * 16 + l16 % 16 >= scnt[p]), NEG, sdead)
        tdead = jnp.where(((r16 % 2) * 4 + l16 // 32 == p) & ((r16 // 2) * 32 + l16 % 32 >= tcnt[p]), NEG, tdead)
    sel[...] = (iota((48, PTS), 0) % 16 == iota((48, PTS), 1) // 128).astype(jnp.bfloat16)

    def spread(rows, dest, halves=(0, 1)):
        parts = jnp.concatenate(thirds(rows), axis=0)
        for half in halves:
            wide = lax.dot_general(
                parts, sel[:, 1024 * half : 1024 * half + 1024], (((0,), (0,)), ((), ())), preferred_element_type=jnp.float32
            )
            for t in range(8):
                dest[pl.ds(1024 * half + 128 * t, 128), :] = wide[:, 128 * t : 128 * t + 128]

    def running(part, block, top, total):
        vs = [block[8 * n : 8 * n + 8, :] + part[8 * n : 8 * n + 8, :] for n in range(16)]
        new = tree(jnp.maximum, vs if top is None else vs + [top])
        more = tree(jnp.add, [jnp.exp2(u - new) for u in vs])
        return new, more if top is None else total * jnp.exp2(top - new) + more

    def close(out, c, top8, total8):
        top = jnp.max(top8, axis=0, keepdims=True)
        total = jnp.sum(total8 * jnp.exp2(top8 - top), axis=0, keepdims=True)
        out[pl.ds(c, 1), :] = top + jnp.log2(total)

    def first(i, carry):
        k = i // 2
        dx = k + (k // 2) * (1 - 2 * (k % 2))

        @pl.when((i % 2 == 0) & (i > 0))
        def _():
            done(xs.at[pl.ds(0, 3)], xsem.at[5 + k, 1])

        c = lax.rem(tx + 4 - dx, 4) * 4 + 2 * (i % 2)
        two = jnp.transpose(xs[pl.ds(c, 2)].reshape(256, 128).astype(jnp.float32)).astype(jnp.bfloat16)
        state = [(None, None)] * 2
        for r in range(8):
            prod = jnp.dot(ys[2 * r : 2 * r + 2].reshape(256, 128), two, preferred_element_type=jnp.float32)
            for v in range(2):
                j = 2 * r + v
                part = gb[pl.ds(128 * j, 128), :]
                for h in range(2):
                    block = SCALE * prod[128 * v : 128 * v + 128, 128 * h : 128 * h + 128] + pt[128 * v : 128 * v + 128, :]
                    rmat[c + h, pl.ds(128 * j, 128), :] = block
                    cmat[j, pl.ds(128 * (c + h), 128), :] = jnp.transpose(block)
                    state[h] = running(part, block, *state[h])
        for h in range(2):
            close(rsend.at[0], c + h, *state[h])
        return carry

    def lse(mat, col, out, lo, hi):
        def step(i, carry):
            state = [(None, None)] * WIDE
            for r in range(PTS // 128):
                part = col[pl.ds(128 * r, 128), :]
                for h in range(WIDE):
                    state[h] = running(part, mat[WIDE * i + h, pl.ds(128 * r, 128), :], *state[h])
            for h in range(WIDE):
                close(out, WIDE * i + h, *state[h])
            return carry

        lax.fori_loop(lo // WIDE, hi // WIDE, step, 0)

    def lse_part(mat, col, out, half):
        def step(i, carry):
            tiles = [WIDE * i + h for h in range(WIDE)]
            state = [(kept[c, 0], kept[c, 1]) if half else (None, None) for c in tiles]
            for r in range(8 * half, 8 * half + 8):
                part = col[pl.ds(128 * r, 128), :]
                for h in range(WIDE):
                    state[h] = running(part, mat[tiles[h], pl.ds(128 * r, 128), :], *state[h])
            for h in range(WIDE):
                if half:
                    close(out, tiles[h], *state[h])
                else:
                    kept[tiles[h], 0] = state[h][0]
                    kept[tiles[h], 1] = state[h][1]
            return carry

        lax.fori_loop(0, TILES // WIDE, step, 0)

    def merge(parts):
        top = tree(jnp.maximum, parts)
        return top + jnp.log2(tree(jnp.add, [jnp.exp2(part - top) for part in parts]))

    for i, n in enumerate(LINE):
        got = tpeer(16 - 4 * n)
        done(sp.at[got], spsem.at[i, 1])
        for m in LINE:
            push(sp.at[got], sp.at[got], spsem.at[3], {"tgt": tpeer(m)})
        piece = tp.at[pl.ds(speer(8 - 2 * n) * 2, 2)]
        done(piece, tpsem.at[i, 1])
        push(piece, piece, tpsem.at[3], {"src": speer(1)})
        done(xs.at[got], xsem.at[i, 1])
        for m in LINE:
            half = xs.at[got, pl.ds(0, 64)]
            push(half, half, xsem.at[6 + i], {"tgt": tpeer(m)})
        got = tpeer(4 - n)
        done(xs.at[got], xsem.at[3 + i, 1])
        for m in LINE:
            half = xs.at[got, pl.ds(64, 64)]
            push(half, half, xsem.at[6 + LINE.index(m)], {"tgt": tpeer(4 * m)})
        piece = ys.at[pl.ds(speer(8 - 2 * n) * 2, 2)]
        done(piece, ysem.at[i, 1])
        push(piece, piece, ysem.at[4], {"src": speer(1)})
    def rows_of(ref, r):
        return jnp.concatenate([ref[t, r : r + 1, :] for t in range(TILES)], axis=0)

    done(tp.at[pl.ds(0, 8)], tpsem.at[3, 1])
    g, lb, yh = rows_of(tp, 0), rows_of(tp, 1), rows_of(tp, 2)
    lb = lb + tdead
    spread(lb + SCALE * (g - yh), gb)
    done(ys.at[pl.ds(0, 2)], ysem.at[3, 1])
    done(ys.at[pl.ds(0, 6)], ysem.at[4, 1])

    def send_rows(k, lo, hi):
        piece = pl.ds(lo, hi - lo)
        rrecv[k, pl.ds(tgt, 1), piece] = rsend[k, piece].reshape(1, hi - lo, 128)
        for d in FAR_T:
            push(rsend.at[k, piece], rrecv.at[k, tgt, piece], rsem.at[k, lo // 8], {"tgt": tpeer(d)})

    def send_cols(k):
        crecv[k, pl.ds(src, 1)] = csend[k].reshape(1, 16, 128)
        for d in FAR_S:
            push(csend.at[k], crecv.at[k, src], csem.at[k], {"src": speer(d)})

    def take_rows(k, f, half):
        piece = pl.ds(8 * half, 8)
        done(rrecv.at[k, pl.ds(0, 15), piece], rsem.at[k, half, 1])
        whole = merge([rrecv[k, i, piece] for i in range(NT)])
        return 0.5 * (f + (xh[8 * half : 8 * half + 8] - whole * (1.0 / SCALE)))

    def take_cols(k, g):
        done(crecv.at[k, pl.ds(0, 7)], csem.at[k, 1])
        return 0.5 * (g + (yh - merge([crecv[k, i] for i in range(NS)]) * (1.0 / SCALE)))

    lax.fori_loop(0, TILES // 2, first, 0)
    send_rows(0, 0, 8)
    send_rows(0, 8, 16)
    done(sp.at[pl.ds(0, 12)], spsem.at[3, 1])
    f, la, xh = rows_of(sp, 0), rows_of(sp, 1), rows_of(sp, 2)
    la = la + sdead
    spread(la + SCALE * (f - xh), fb)
    f = [f[0:8], f[8:16]]
    lse(cmat, fb, csend.at[0], 0, 16)
    send_cols(0)
    ytr[128:144, :] = jnp.ones((16, PTS), jnp.bfloat16)
    for t in range(TILES):
        ytr[0:128, pl.ds(128 * t, 128)] = jnp.transpose(ys[t].astype(jnp.float32)).astype(jnp.bfloat16)

    def row_half(k, g):
        g = take_cols(k - 1, g)
        spread(lb + SCALE * (g - yh), gb)
        for lo in (0, 8):
            lse(rmat, gb, rsend.at[k], lo, lo + 8)
            send_rows(k, lo, lo + 8)
        return g

    def col_half(k, f):
        f = list(f)
        for half in range(2):
            f[half] = take_rows(k - 1, f[half], half)
            at = slice(8 * half, 8 * half + 8)
            rows = la[at] + SCALE * (f[half] - xh[at])
            zero = jnp.zeros((8, 128), jnp.float32)
            spread(jnp.concatenate([zero, rows] if half else [rows, zero], axis=0), fb, (half,))
            lse_part(cmat, fb, csend.at[k], half)
        send_cols(k)
        return f

    for k in range(1, ITERS):
        if k % 2:
            f = col_half(k, f)
            g = row_half(k, g)
        else:
            g = row_half(k, g)
            f = col_half(k, f)
    g = take_cols(ITERS - 1, g)
    spread(lb + SCALE * (g - yh), gb)

    def project(i, carry):
        ds = [15 - 2 * i, 14 - 2 * i]
        cs = [lax.rem(tx + lax.div(d, 4), 4) * 4 + lax.rem(ty + lax.rem(d, 4), 4) for d in ds]
        tops = [[], []]
        for r in range(16):
            part = gb[pl.ds(128 * r, 128), :]
            for h in range(2):
                v = rmat[cs[h], pl.ds(128 * r, 128), :] + part
                vbuf[h, pl.ds(128 * r, 128), :] = v
                tops[h].append(fold(jnp.maximum, v))
        tops = [jnp.max(tree(jnp.maximum, t), axis=0, keepdims=True) for t in tops]
        for r in range(16):
            for h in range(2):
                w = jnp.exp2(vbuf[h, pl.ds(128 * r, 128), :] - tops[h])
                high = w.astype(jnp.bfloat16)
                whi[pl.ds(128 * r, 128), 128 * h : 128 * h + 128] = high
                wlo[pl.ds(128 * r, 128), 128 * h : 128 * h + 128] = (w - high.astype(jnp.float32)).astype(jnp.bfloat16)
        moved = jnp.dot(ytr[...], whi[...], preferred_element_type=jnp.float32) + jnp.dot(
            ytr[...], wlo[...], preferred_element_type=jnp.float32
        )
        r8 = iota((8, 128), 0)
        for h in range(2):
            block = moved[0:128, 128 * h : 128 * h + 128]
            most = jnp.max(fold(jnp.maximum, jnp.abs(block)), axis=0, keepdims=True)
            most = jnp.maximum(most, 1e-30)
            msg[ds[h]] = jnp.round(block * (32767.0 / most)).astype(jnp.int32).astype(jnp.int16)
            rows = (tops[h], moved[128:129, 128 * h : 128 * h + 128], most * (1.0 / 32767.0))
            stat[ds[h]] = tree(jnp.add, [jnp.where(r8 == n, jnp.broadcast_to(row, (8, 128)), 0.0) for n, row in enumerate(rows)])
        push(stat.at[ds[0]], srecv.at[ds[0]], ssem, {"tgt": cs[0]})
        push(msg.at[ds[0]], mrecv.at[ds[0]], msem, {"tgt": cs[0]})

        @pl.when(ds[1] > 0)
        def _():
            push(stat.at[ds[1]], srecv.at[ds[1]], ssem, {"tgt": cs[1]})
            push(msg.at[ds[1]], mrecv.at[ds[1]], msem, {"tgt": cs[1]})

        return carry

    lax.fori_loop(0, 8, project, 0)
    for half in range(2):
        fb[8 * half : 8 * half + 8, :] = take_rows(ITERS - 1, f[half], half)
    f_out[...] = from_lanes(fb[pl.ds(tgt, 1), :], 16)
    gb[0:16, :] = g
    g_out[...] = from_lanes(gb[pl.ds(src * 2, 2), :], 32)
    mrecv[0] = msg[0]
    srecv[0] = stat[0]
    done(srecv.at[pl.ds(1, 15)], ssem.at[1])
    tops = [srecv[d, 0:1, :] for d in range(16)]
    top = tree(jnp.maximum, tops)
    scales = [jnp.exp2(t - top) for t in tops]
    inv = 1.0 / tree(jnp.add, [scales[d] * srecv[d, 1:2, :] for d in range(16)])
    scales = [scales[d] * srecv[d, 2:3, :] * inv for d in range(16)]
    done(mrecv.at[pl.ds(1, 15)], msem.at[1])
    moved = tree(jnp.add, [scales[d] * mrecv[d].astype(jnp.int32).astype(jnp.float32) for d in range(16)])
    img_out[...] = jnp.transpose(moved)

    for i in range(6):
        done(xs.at[0], xsem.at[i, 0])
    for i in range(3):
        done(xs.at[pl.ds(0, 3)], xsem.at[6 + i, 0])
    for i in range(4):
        done(ys.at[pl.ds(0, 2)], ysem.at[i, 0])
    done(ys.at[pl.ds(0, 6)], ysem.at[4, 0])
    for i in range(3):
        done(sp.at[0], spsem.at[i, 0])
        done(tp.at[pl.ds(0, 2)], tpsem.at[i, 0])
    done(sp.at[pl.ds(0, 12)], spsem.at[3, 0])
    done(tp.at[pl.ds(0, 8)], tpsem.at[3, 0])
    for k in range(ITERS):
        for half in range(2):
            done(rrecv.at[k, pl.ds(0, 15), pl.ds(8 * half, 8)], rsem.at[k, half, 0])
        done(crecv.at[k, pl.ds(0, 7)], csem.at[k, 0])
    done(mrecv.at[pl.ds(1, 15)], msem.at[0])
    done(srecv.at[pl.ds(1, 15)], ssem.at[0])


def on_device(src_points, tgt_points, src_mass, tgt_mass, src_potential, tgt_potential, src_counts, tgt_counts, keep):
    f32, bf16 = jnp.float32, jnp.bfloat16
    vmem = pl.BlockSpec(memory_space=pltpu.VMEM)
    smem = pl.BlockSpec(memory_space=pltpu.SMEM)
    dma = pltpu.SemaphoreType.DMA
    images, f, g = pl.pallas_call(
        kernel,
        out_shape=(
            jax.ShapeDtypeStruct((128, 128), f32),
            jax.ShapeDtypeStruct((8, 16), f32),
            jax.ShapeDtypeStruct((8, 32), f32),
        ),
        in_specs=[smem] * 3 + [vmem] * 6,
        out_specs=(vmem, vmem, vmem),
        scratch_shapes=[
            pltpu.VMEM((16, 128, 128), bf16),
            pltpu.VMEM((16, 128, 128), bf16),
            pltpu.VMEM((16, 8, 128), f32),
            pltpu.VMEM((16, 8, 128), f32),
            pltpu.VMEM((144, PTS), bf16),
            pltpu.VMEM((16, PTS, 128), f32),
            pltpu.VMEM((16, PTS, 128), f32),
            pltpu.VMEM((2, PTS, 128), f32),
            pltpu.VMEM((PTS, 128), f32),
            pltpu.VMEM((PTS, 128), f32),
            pltpu.VMEM((48, PTS), bf16),
            pltpu.VMEM((256, 128), f32),
            pltpu.VMEM((PTS, 256), bf16),
            pltpu.VMEM((PTS, 256), bf16),
            pltpu.VMEM((8, 128), f32),
            pltpu.VMEM((2, 8, 128), f32),
            pltpu.VMEM((ITERS, 16, 128), f32),
            pltpu.VMEM((ITERS, 16, 16, 128), f32),
            pltpu.VMEM((ITERS, 16, 128), f32),
            pltpu.VMEM((ITERS, 8, 16, 128), f32),
            pltpu.VMEM((16, 128, 128), jnp.int16),
            pltpu.VMEM((16, 128, 128), jnp.int16),
            pltpu.VMEM((16, 8, 128), f32),
            pltpu.VMEM((16, 8, 128), f32),
            dma((9, 2)),
            dma((4, 2)),
            dma((5, 2)),
            dma((4, 2)),
            dma((ITERS, 2, 2)),
            dma((ITERS, 2)),
            dma((2,)),
            dma((2,)),
            pltpu.VMEM((TILES, 2, 8, 128), f32),
        ],
        compiler_params=pltpu.CompilerParams(
            collective_id=0, has_side_effects=True, vmem_limit_bytes=60 * 1024 * 1024
        ),
        name="sinkhorn",
    )(
        src_counts,
        tgt_counts,
        keep,
        src_points.reshape(128, 128),
        tgt_points.reshape(2, 128, 128),
        src_mass,
        tgt_mass,
        src_potential,
        tgt_potential,
    )
    return images.reshape(8, 16, 128), f, g


def solution(mesh):
    return jax.shard_map(
        on_device,
        mesh=mesh,
        in_specs=(
            P("src", "tgt", None),
            P("tgt", "src", None),
            P("src", "tgt"),
            P("tgt", "src"),
            P("src", "tgt"),
            P("tgt", "src"),
            P("src"),
            P("tgt"),
            P("src", "tgt"),
        ),
        out_specs=(P("src", "tgt", None), P("src", "tgt"), P("tgt", "src")),
        check_vma=False,
    )
```

time: 77.9 us -> 70.5 us (0.905)
  Pallas kernels: 74.3 us -> 66.9 us
    pallas_call x1, Pallas kernels: 74.3 us -> 66.9 us  [on_device(): pl.pallas_call(kernel, out_shape=(jax.ShapeDtypeStruct((128, 128), f32),...]
where the time goes in v3:
time: 70.5 us; the launch traced here: 70.3 us
  Pallas kernels  66.9 us (95%)
  local copies, waits for them, and re-layouts  2.74 us (4%)
    pallas_call x1, Pallas kernels, on_device(): pl.pallas_call(kernel, out_shape=(jax.ShapeDtypeStruct((128, 128), f32),...  66.9 us
    unnamed x7, local copies, waits for them, and re-layouts  2.74 us

profile of v3, /device:TPU:1, one launch (start us, length us, event | category | flops | bytes accessed | tf_op | source)
XLA Modules:
  0.0 70.3 jit_solution(12250892351325911025)
XLA Ops:
  0.6 66.9 %sinkhorn.1 = (f32[128,128]{1,0:T(8,128)}, f32[8,16]{1,0:T(8,128)}, f32[8,32]{1,0:T(8,128)}) custom-call(s32[8]{0:T(128)} %scnt.1, s32[8]{0:T(128)} %tcnt.1, s32[8,8]{1,0:T(8,128)} %keep.1, bf16[128,128]{1,0:T(8,128)(2,1)} %bitcast.5, bf16[2,128,128]{2,1,0:T(8,128)(2,1)} %bitcast.3, bf16[8,16]{1,0:T(8,128)(2,1)} %a_in.1, bf16[8,32]{1,0:T(8,128)(2,1)} %b_in.1, ...), custom_call_target="tpu_custom_call" | custom-call | tf_op jit(solution)/shard_map/sinkhorn/pallas_call | solution.py:408
  67.6 0.0 copy-start.1
  67.6 1.5 %copy.15 = f32[8,16,128]{2,1,0:T(8,128)} copy(f32[8,16,128]{2,1,0:T(8,128)} %bitcast.4) | data formatting | bytes 131072
  69.0 0.0 copy-done.1
  69.0 0.0 copy-start
  69.0 0.6 copy.16
  69.6 0.1 copy-done
  69.7 0.6 copy.17
Async XLA Ops:
  67.6 1.5 %copy-start.1 = (f32[8,16]{1,0:T(8,128)S(1)}, f32[8,16]{1,0:T(8,128)}, u32[]{:S(2)}) copy-start(f32[8,16]{1,0:T(8,128)} %get-tuple-element.13) | copy-start | bytes 1540
  69.0 0.7 copy-start

commit v4 on v3

--- a/solution.py
+++ b/solution.py
@@ -19,11 +19,16 @@
 WIDE = 4
 FAR_T = sorted(range(1, NT), key=lambda d: -(min(d // 4, 4 - d // 4) + min(d % 4, 4 - d % 4)))
 LINE = (1, 3, 2)
+ORDER = FAR_T + [0]
 FAR_S = sorted(range(1, NS), key=lambda d: -(2 * min(d // 2, 4 - d // 2) + d % 2))
 
 
 def iota(shape, dim):
     return lax.broadcasted_iota(jnp.int32, shape, dim)
+
+
+def pick(i, values):
+    return sum(jnp.where(i == n, v, 0) for n, v in enumerate(values))
 
 
 def tree(op, parts):
@@ -237,6 +242,9 @@
         piece = tp.at[pl.ds(speer(8 - 2 * n) * 2, 2)]
         done(piece, tpsem.at[i, 1])
         push(piece, piece, tpsem.at[3], {"src": speer(1)})
+        piece = ys.at[pl.ds(speer(8 - 2 * n) * 2, 2)]
+        done(piece, ysem.at[i, 1])
+        push(piece, piece, ysem.at[4], {"src": speer(1)})
         done(xs.at[got], xsem.at[i, 1])
         for m in LINE:
             half = xs.at[got, pl.ds(0, 64)]
@@ -246,9 +254,6 @@
         for m in LINE:
             half = xs.at[got, pl.ds(64, 64)]
             push(half, half, xsem.at[6 + LINE.index(m)], {"tgt": tpeer(4 * m)})
-        piece = ys.at[pl.ds(speer(8 - 2 * n) * 2, 2)]
-        done(piece, ysem.at[i, 1])
-        push(piece, piece, ysem.at[4], {"src": speer(1)})
     def rows_of(ref, r):
         return jnp.concatenate([ref[t, r : r + 1, :] for t in range(TILES)], axis=0)
 
@@ -325,22 +330,22 @@
     spread(lb + SCALE * (g - yh), gb)
 
     def project(i, carry):
-        ds = [15 - 2 * i, 14 - 2 * i]
+        ds = [pick(i, ORDER[0::2]), pick(i, ORDER[1::2])]
         cs = [lax.rem(tx + lax.div(d, 4), 4) * 4 + lax.rem(ty + lax.rem(d, 4), 4) for d in ds]
         tops = [[], []]
         for r in range(16):
             part = gb[pl.ds(128 * r, 128), :]
             for h in range(2):
                 v = rmat[cs[h], pl.ds(128 * r, 128), :] + part
-                vbuf[h, pl.ds(128 * r, 128), :] = v
                 tops[h].append(fold(jnp.maximum, v))
         tops = [jnp.max(tree(jnp.maximum, t), axis=0, keepdims=True) for t in tops]
         for r in range(16):
+            part = gb[pl.ds(128 * r, 128), :]
             for h in range(2):
-                w = jnp.exp2(vbuf[h, pl.ds(128 * r, 128), :] - tops[h])
-                high = w.astype(jnp.bfloat16)
-                whi[pl.ds(128 * r, 128), 128 * h : 128 * h + 128] = high
-                wlo[pl.ds(128 * r, 128), 128 * h : 128 * h + 128] = (w - high.astype(jnp.float32)).astype(jnp.bfloat16)
+                w = jnp.exp2((rmat[cs[h], pl.ds(128 * r, 128), :] + part) - tops[h])
+                at = (pl.ds(128 * r, 128), slice(128 * h, 128 * h + 128))
+                whi[at] = w.astype(jnp.bfloat16)
+                wlo[at] = (w - whi[at].astype(jnp.float32)).astype(jnp.bfloat16)
         moved = jnp.dot(ytr[...], whi[...], preferred_element_type=jnp.float32) + jnp.dot(
             ytr[...], wlo[...], preferred_element_type=jnp.float32
         )

time: 70.5 us -> 68 us (0.965)
  Pallas kernels: 66.9 us -> 64.4 us
    pallas_call x1, Pallas kernels: 66.9 us -> 64.4 us  [on_device(): pl.pallas_call(kernel, out_shape=(jax.ShapeDtypeStruct((128, 128), f32),...]
where the time goes in v4:
time: 68 us; the launch traced here: 67.8 us
  Pallas kernels  64.4 us (95%)
  local copies, waits for them, and re-layouts  2.74 us (4%)
    pallas_call x1, Pallas kernels, on_device(): pl.pallas_call(kernel, out_shape=(jax.ShapeDtypeStruct((128, 128), f32),...  64.4 us
    unnamed x7, local copies, waits for them, and re-layouts  2.74 us

profile of v4, /device:TPU:1, one launch (start us, length us, event | category | flops | bytes accessed | tf_op | source)
XLA Modules:
  0.0 67.8 jit_solution(12654649504355928740)
XLA Ops:
  0.6 64.4 %sinkhorn.1 = (f32[128,128]{1,0:T(8,128)}, f32[8,16]{1,0:T(8,128)}, f32[8,32]{1,0:T(8,128)}) custom-call(s32[8]{0:T(128)} %scnt.1, s32[8]{0:T(128)} %tcnt.1, s32[8,8]{1,0:T(8,128)} %keep.1, bf16[128,128]{1,0:T(8,128)(2,1)} %bitcast.5, bf16[2,128,128]{2,1,0:T(8,128)(2,1)} %bitcast.3, bf16[8,16]{1,0:T(8,128)(2,1)} %a_in.1, bf16[8,32]{1,0:T(8,128)(2,1)} %b_in.1, ...), custom_call_target="tpu_custom_call" | custom-call | tf_op jit(solution)/shard_map/sinkhorn/pallas_call | solution.py:413
  65.0 0.0 copy-start.1
  65.0 1.5 %copy.15 = f32[8,16,128]{2,1,0:T(8,128)} copy(f32[8,16,128]{2,1,0:T(8,128)} %bitcast.4) | data formatting | bytes 131072
  66.5 0.0 copy-done.1
  66.5 0.0 copy-start
  66.5 0.6 copy.16
  67.1 0.1 copy-done
  67.2 0.6 copy.17
Async XLA Ops:
  65.0 1.5 %copy-start.1 = (f32[8,16]{1,0:T(8,128)S(1)}, f32[8,16]{1,0:T(8,128)}, u32[]{:S(2)}) copy-start(f32[8,16]{1,0:T(8,128)} %get-tuple-element.13) | copy-start | bytes 1540
  66.5 0.7 copy-start

commit v5 on v4

--- a/solution.py
+++ b/solution.py
@@ -193,7 +193,8 @@
                 for h in range(2):
                     block = SCALE * prod[128 * v : 128 * v + 128, 128 * h : 128 * h + 128] + pt[128 * v : 128 * v + 128, :]
                     rmat[c + h, pl.ds(128 * j, 128), :] = block
-                    cmat[j, pl.ds(128 * (c + h), 128), :] = jnp.transpose(block)
+                    if v == 0:
+                        cmat[j, pl.ds(128 * (c + h), 128), :] = jnp.transpose(block)
                     state[h] = running(part, block, *state[h])
         for h in range(2):
             close(rsend.at[0], c + h, *state[h])
@@ -211,6 +212,22 @@
             return carry
 
         lax.fori_loop(lo // WIDE, hi // WIDE, step, 0)
+
+    def first_cols(i, carry):
+        state = [(None, None)] * WIDE
+        for r in range(TILES):
+            part = fb[pl.ds(128 * r, 128), :]
+            for h in range(WIDE):
+                c = WIDE * i + h
+                if h % 2:
+                    block = jnp.transpose(rmat[r, pl.ds(128 * c, 128), :])
+                    cmat[c, pl.ds(128 * r, 128), :] = block
+                else:
+                    block = cmat[c, pl.ds(128 * r, 128), :]
+                state[h] = running(part, block, *state[h])
+        for h in range(WIDE):
+            close(csend.at[0], WIDE * i + h, *state[h])
+        return carry
 
     def lse_part(mat, col, out, half):
         def step(i, carry):
@@ -293,7 +310,7 @@
     la = la + sdead
     spread(la + SCALE * (f - xh), fb)
     f = [f[0:8], f[8:16]]
-    lse(cmat, fb, csend.at[0], 0, 16)
+    lax.fori_loop(0, TILES // WIDE, first_cols, 0)
     send_cols(0)
     ytr[128:144, :] = jnp.ones((16, PTS), jnp.bfloat16)
     for t in range(TILES):
@@ -308,14 +325,9 @@
         return g
 
     def col_half(k, f):
-        f = list(f)
-        for half in range(2):
-            f[half] = take_rows(k - 1, f[half], half)
-            at = slice(8 * half, 8 * half + 8)
-            rows = la[at] + SCALE * (f[half] - xh[at])
-            zero = jnp.zeros((8, 128), jnp.float32)
-            spread(jnp.concatenate([zero, rows] if half else [rows, zero], axis=0), fb, (half,))
-            lse_part(cmat, fb, csend.at[k], half)
+        f = [take_rows(k - 1, f[half], half) for half in range(2)]
+        spread(la + SCALE * (jnp.concatenate(f, axis=0) - xh), fb)
+        lse(cmat, fb, csend.at[k], 0, 16)
         send_cols(k)
         return f
 

time: 68 us -> 66.2 us (0.974)
  Pallas kernels: 64.4 us -> 62.6 us
    pallas_call x1, Pallas kernels: 64.4 us -> 62.6 us  [on_device(): pl.pallas_call(kernel, out_shape=(jax.ShapeDtypeStruct((128, 128), f32),...]
where the time goes in v5:
time: 66.2 us; the launch traced here: 66 us
  Pallas kernels  62.6 us (95%)
  local copies, waits for them, and re-layouts  2.74 us (4%)
    pallas_call x1, Pallas kernels, on_device(): pl.pallas_call(kernel, out_shape=(jax.ShapeDtypeStruct((128, 128), f32),...  62.6 us
    unnamed x7, local copies, waits for them, and re-layouts  2.74 us

profile of v5, /device:TPU:1, one launch (start us, length us, event | category | flops | bytes accessed | tf_op | source)
XLA Modules:
  0.0 66.0 jit_solution(9790322486022109435)
XLA Ops:
  0.6 62.6 %sinkhorn.1 = (f32[128,128]{1,0:T(8,128)}, f32[8,16]{1,0:T(8,128)}, f32[8,32]{1,0:T(8,128)}) custom-call(s32[8]{0:T(128)} %scnt.1, s32[8]{0:T(128)} %tcnt.1, s32[8,8]{1,0:T(8,128)} %keep.1, bf16[128,128]{1,0:T(8,128)(2,1)} %bitcast.5, bf16[2,128,128]{2,1,0:T(8,128)(2,1)} %bitcast.3, bf16[8,16]{1,0:T(8,128)(2,1)} %a_in.1, bf16[8,32]{1,0:T(8,128)(2,1)} %b_in.1, ...), custom_call_target="tpu_custom_call" | custom-call | tf_op jit(solution)/shard_map/sinkhorn/pallas_call | solution.py:425
  63.2 0.0 copy-start.1
  63.2 1.5 %copy.15 = f32[8,16,128]{2,1,0:T(8,128)} copy(f32[8,16,128]{2,1,0:T(8,128)} %bitcast.4) | data formatting | bytes 131072
  64.7 0.0 copy-done.1
  64.7 0.0 copy-start
  64.7 0.6 copy.16
  65.3 0.1 copy-done
  65.4 0.6 copy.17
Async XLA Ops:
  63.2 1.5 %copy-start.1 = (f32[8,16]{1,0:T(8,128)S(1)}, f32[8,16]{1,0:T(8,128)}, u32[]{:S(2)}) copy-start(f32[8,16]{1,0:T(8,128)} %get-tuple-element.13) | copy-start | bytes 1540
  64.7 0.7 %copy-start = (f32[8,32]{1,0:T(8,128)S(1)}, f32[8,32]{1,0:T(8,128)}, u32[]{:S(2)}) copy-start(f32[8,32]{1,0:T(8,128)} %get-tuple-element.14) | copy-start | bytes 3076
